TPU v7x, 256 devices: a whole 4x4x8 slice. The times are simulated.
256 devices in a mesh: freq: 8 (over z_hi, core), frames: 32 (over z_lo, x, y).
Axes of the slice: x: 4, y: 4, z: 8 (z_hi: 4, z_lo: 2; z = z_hi * 2 + z_lo), core: 2. Of those that a mesh axis runs over, the one named last changes fastest.
Arguments:
- signal: float32 [32, 8, 1048576], P('frames', 'freq'), may hold values from -6 to 6
- templates: float32 [64, 32768], P(None, ('freq', 'frames')), may hold values from 0.03 to 3.6, as said below
- activations: float32 [64, 8192], P('freq', 'frames'), may hold values from 0.3 to 36, as said below
Outputs:
- final_activations: float32 [64, 8192], P('freq', 'frames')
- final_templates: float32 [64, 32768], P(None, ('freq', 'frames'))
Inputs may be any that keep to these rules, and one draw needn't show every extreme that they name: `templates`: all entries are positive. `activations`: all entries are positive.
All inputs are finite; a program needn't handle non-finite values.
Results may differ from a plain program's by a relative error of at most 0.00011.
Values sent between devices are 32-bit elements; how exact they have to be, the bound alone decides.
A program may use at most 64 MiB of HBM per device.

v0:
```python
import math

import jax
import jax.numpy as jnp
from jax import lax
from jax.sharding import PartitionSpec as P

FRAME_LEN = 65536
SPLIT = 256


PRECISE = lax.Precision.HIGHEST


def passed_along(block, axis, distance):
    devices = range(lax.axis_size(axis))
    route = [((i - distance) % len(devices), i) for i in devices]
    return lax.ppermute(block, axis, route)


def from_behind(value, axis, steps):
    count = lax.axis_size(axis)
    leading, last = (max(0, -steps), min(count, count - steps))
    return lax.ppermute(value, axis, [(source, source + steps) for source in range(leading, last)])


def hann_window():
    positions = jnp.arange(FRAME_LEN, dtype=jnp.int32).astype(jnp.float32)
    return 0.5 - 0.5 * jnp.cos(2.0 * math.pi / FRAME_LEN * positions)


def fourier_tables(split_len):
    indices = jnp.arange(split_len, dtype=jnp.int32)
    products = indices[:, None] * indices[None, :] % split_len
    angles = 2.0 * math.pi / split_len * products.astype(jnp.float32)
    cosine_table = jnp.cos(angles)
    sine_table = jnp.sin(angles)
    first_section = jnp.concatenate([cosine_table, -sine_table], 0)
    half_split = split_len // 2
    cos_half = cosine_table[:half_split]
    sin_half = sine_table[:half_split]
    second_section = jnp.concatenate(
        [jnp.concatenate([cos_half, sin_half], 1), jnp.concatenate([-sin_half, cos_half], 1)], 0
    )
    twiddle = (
        2.0
        * math.pi
        / (split_len * split_len)
        * (indices[:, None] * indices[None, :]).astype(jnp.float32)
    )
    return (first_section, second_section, jnp.cos(twiddle), jnp.sin(twiddle))


def frame_magnitudes(extended, frame_count):
    first_section, second_section, twiddle_cos, twiddle_sin = fourier_tables(SPLIT)
    window = hann_window()
    group_size = math.gcd(frame_count, 4)
    half_split = SPLIT // 2

    def per_block(offset):
        first_half = lax.dynamic_slice_in_dim(extended, offset, group_size, 0)
        second_half = lax.dynamic_slice_in_dim(extended, offset + 1, group_size, 0)
        frames = jnp.concatenate([first_half, second_half], 1) * window
        samples = frames.reshape(group_size, SPLIT, SPLIT)
        section_one = jnp.einsum(
            "oq,gqp->gop",
            first_section,
            samples,
            precision=PRECISE,
            preferred_element_type=jnp.float32,
        )
        real_one = section_one[:, :SPLIT]
        imag_one = section_one[:, SPLIT:]
        twisted = jnp.concatenate(
            [
                real_one * twiddle_cos + imag_one * twiddle_sin,
                imag_one * twiddle_cos - real_one * twiddle_sin,
            ],
            2,
        )
        section_two = jnp.einsum(
            "oc,gjc->goj",
            second_section,
            twisted,
            precision=PRECISE,
            preferred_element_type=jnp.float32,
        )
        real_two = section_two[:, :half_split]
        imag_two = section_two[:, half_split:]
        magnitude = jnp.sqrt(real_two * real_two + imag_two * imag_two) * (8.0 / SPLIT)
        return magnitude.reshape(group_size, half_split * SPLIT)

    offsets = jnp.arange(frame_count // group_size, dtype=jnp.int32) * group_size
    return lax.map(per_block, offsets).reshape(frame_count, half_split * SPLIT)


def gather_basis(own_columns):
    return lax.all_gather(own_columns, "frames", axis=1, tiled=True)


def gather_activity(own_rows):
    return lax.all_gather(own_rows, "freq", axis=0, tiled=True)


def quotient(spectrum, basis_full, act_full):
    approx = lax.dot_general(
        act_full,
        basis_full,
        (((0,), (0,)), ((), ())),
        precision=PRECISE,
        preferred_element_type=jnp.float32,
    )
    return spectrum / approx


def update_activity(spectrum, basis_full, act_full, act_own, want_full):
    ratio_rows = quotient(spectrum, basis_full, act_full)
    numerator = lax.dot_general(
        basis_full,
        ratio_rows,
        (((1,), (1,)), ((), ())),
        precision=PRECISE,
        preferred_element_type=jnp.float32,
    )
    totals = jnp.sum(basis_full, axis=1)
    numerator, totals = (
        lax.psum_scatter(numerator, "freq", scatter_dimension=0, tiled=True),
        lax.psum_scatter(totals[:, None], "freq", scatter_dimension=0, tiled=True),
    )
    new_own = act_own * (numerator / totals)
    if want_full:
        return (new_own, gather_activity(new_own))
    return (new_own, new_own)


def on_device(signal, templates, activations):
    hop_len = FRAME_LEN // 2
    sample_rows = signal.reshape(-1, hop_len)
    frame_count = sample_rows.shape[0]
    leading = sample_rows[:1]
    from_next = passed_along(leading, "freq", -1)
    from_later = from_behind(from_next, "frames", -1)
    last_sub = lax.axis_index("freq") == lax.axis_size("freq") - 1
    trailing = jnp.where(last_sub, from_later, from_next)
    extended = jnp.concatenate([sample_rows, trailing], 0)
    spectrum = frame_magnitudes(extended, frame_count)
    spectrum = lax.all_to_all(spectrum, "freq", split_axis=1, concat_axis=0, tiled=True)
    basis_full = gather_basis(templates)
    act_full = gather_activity(activations)
    middle_own, middle_full = update_activity(spectrum, basis_full, act_full, activations, True)
    second_ratio = quotient(spectrum, basis_full, middle_full)
    numerator = jnp.dot(
        middle_full, second_ratio, precision=PRECISE, preferred_element_type=jnp.float32
    )
    totals = jnp.sum(middle_full, axis=1)
    numerator = lax.psum_scatter(numerator, "frames", scatter_dimension=1, tiled=True)
    totals = lax.psum(totals, "frames")
    basis_own = templates * (numerator / totals[:, None])
    new_basis = gather_basis(basis_own)
    final_own, unused = update_activity(spectrum, new_basis, middle_full, middle_own, False)
    return (final_own, basis_own)


def solution(mesh):
    return jax.shard_map(
        on_device,
        mesh=mesh,
        in_specs=(P("frames", "freq", None), P(None, ("freq", "frames")), P("freq", "frames")),
        out_specs=(P("freq", "frames"), P(None, ("freq", "frames"))),
        check_vma=False,
    )
```

profile of v0, /device:TPU:1, one launch (start us, length us, event | category | flops | bytes accessed | tf_op | source)
XLA Modules:
  0.0 784.9 jit_solution(11796974284045732017)
XLA Ops:
  17.0 34.1 %reduce.3 = f32[1048576]{0:T(1024)} reduce(f32[1,1,1048576]{2,1,0:T(1,128)} %param.5, f32[]{:T(128)} %broadcast.48), dimensions={0,1}, to_apply=%param.5.reduce_sub_computation.3 | reduce | bytes 8388612 | tf_op args[0]
  51.1 5.0 reshape.36
  56.4 4.9 pad_maximum_fusion
  61.2 137.7 %while.14 = (s32[]{:T(128)}, f32[8,4,32768]{2,1,0:T(4,128)}, s32[8]{0:T(128)S(1)}, f32[33,32768]{1,0:T(8,128)}, f32[512,256]{1,0:T(8,128)S(1)}, /*index=5*/f32[2...) while((s32[]{:T(128)}, f32[8,4,32768]{2,1,0:T(4,128)}, ...), condition=%wide.region_1.2_spmd.clone.clone, body=%wide.region_0.1_spmd.clone.clone.sunk | while | flops 3224829952 | bytes 22545096 | solution.py:94
  73.8 3.5 fusion.61
  86.3 3.4 convolution_bitcast_fusion.3
  91.0 3.5 fusion.61
  108.1 3.5 fusion.61
  125.2 3.5 fusion.61
  142.4 3.5 fusion.61
  159.5 3.5 fusion.61
  176.7 3.5 fusion.61
  193.9 3.5 fusion.61
  199.0 6.2 all_to_all.14
  205.2 6.6 copy.16
  211.8 9.5 %all-to-all-start = ((f32[32,8,4096]{2,0,1:T(8,128)}), f32[32,8,4096]{2,0,1:T(8,128)}, u32[]{:S(2)}, u32[]{:S(2)}) async-start(f32[32,8,4096]{2,0,1:T(8,128)} %copy.16), calls=%async_computation | async-start | bytes 8388608 | tf_op jit(solution)/shard_map/all_to_all | solution.py:147
  222.1 108.5 %all_gather.12 = f32[64,256]{1,0:T(8,128)S(1)} all-gather(f32[8,256]{1,0:T(8,128)S(1)} %copy-done.3), channel_id=1, replica_groups=mesh['freq'=8,'frames'=32] {'freq'}, dimensions={0}, use_global_device_ids=true | all-gather | bytes 73728 | tf_op jit(solution)/shard_map/all_gather | solution.py:102
  330.6 27.5 %all-gather.3.cloned.1.call-done = f32[64,4096]{1,0:T(8,128)} async-done(((f32[64,128]{1,0:T(8,128)}), f32[64,4096]{1,0:T(8,128)}) %all-gather.3.cloned.1.call-update) | async-done | bytes 1048592 | tf_op jit(solution)/shard_map/all_gather | solution.py:98
  358.1 6.2 convolution_divide_fusion.2
  364.3 4.6 convolution_bitcast_fusion.1
  370.3 29.7 %all-reduce = f32[64,1]{0,1:T(1,128)S(1)} all-reduce(f32[64,1]{0,1:T(1,128)S(1)} %bitcast.66), channel_id=3, replica_groups=mesh['freq'=8,'frames'=32] {'freq'}, use_global_device_ids=true, to_apply=%region_4.5.clone | all-reduce | flops 64 | bytes 512
  400.1 19.9 %reduce-scatter.6.cloned.1.call-done = f32[8,256]{1,0:T(8,128)} async-done(((f32[64,256]{1,0:T(8,128)}), f32[8,256]{1,0:T(8,128)}) %reduce-scatter.6.cloned.1.call-update) | async-done | bytes 8208 | tf_op jit(solution)/shard_map/reduce_scatter | solution.py:127
  420.8 16.8 %all_gather.14 = f32[64,256]{1,0:T(8,128)S(1)} all-gather(f32[8,256]{1,0:T(8,128)S(1)} %divide_multiply_fusion.2), channel_id=1, replica_groups=mesh['freq'=8,'frames'=32] {'freq'}, dimensions={0}, use_global_device_ids=true | all-gather | bytes 73728 | tf_op jit(solution)/shard_map/all_gather | solution.py:102
  437.6 5.7 convolution_divide_fusion.1
  443.3 3.6 fusion.37
  447.1 68.7 %psum.7 = f32[64]{0:T(128)S(1)} all-reduce(f32[64]{0:T(128)S(1)} %reduce_sum.28), channel_id=1, replica_groups=mesh['freq'=8,'frames'=32] {'frames'}, use_global_device_ids=true, to_apply=%region_7.8 | all-reduce | flops 64 | bytes 512 | tf_op jit(solution)/shard_map/psum | solution.py:157
  515.8 68.4 %reduce-scatter.8.cloned.1.call-done = f32[64,128]{1,0:T(8,128)} async-done(((f32[64,4096]{1,0:T(8,128)}), f32[64,128]{1,0:T(8,128)}) %reduce-scatter.8.cloned.1.call-update) | async-done | bytes 32784 | tf_op jit(solution)/shard_map/reduce_scatter | solution.py:156
  585.7 127.6 %all-gather.5.cloned.1.call-done = f32[64,4096]{1,0:T(8,128)} async-done(((f32[64,128]{1,0:T(8,128)}), f32[64,4096]{1,0:T(8,128)}) %all-gather.5.cloned.1.call-update) | async-done | bytes 1048592 | tf_op jit(solution)/shard_map/all_gather | solution.py:98
  713.3 6.2 convolution_divide_fusion
  719.5 4.6 fusion.38
  724.3 31.5 %all-reduce.1 = f32[64,1]{0,1:T(1,128)S(1)} all-reduce(f32[64,1]{0,1:T(1,128)S(1)} %bitcast.65), channel_id=6, replica_groups=mesh['freq'=8,'frames'=32] {'freq'}, use_global_device_ids=true, to_apply=%region_10.11.clone | all-reduce | flops 64 | bytes 512
  755.9 20.8 %reduce-scatter.10.cloned.1.call-done = f32[8,256]{1,0:T(8,128)} async-done(((f32[64,256]{1,0:T(8,128)}), f32[8,256]{1,0:T(8,128)}) %reduce-scatter.10.cloned.1.call-update) | async-done | bytes 8208 | tf_op jit(solution)/shard_map/reduce_scatter | solution.py:127
  (140 shorter events, 94.9 us)
Async XLA Ops:
  8.1 7.1 collective-permute-start
  15.2 41.0 %collective-permute-start.1 = (f32[1,32768]{1,0:T(1,128)S(1)}, f32[1,32768]{1,0:T(1,128)S(1)}, u32[]{:S(2)}, u32[]{:S(2)}) collective-permute-start(f32[1,32768]{1,0:T(1,128)S(1)} %collective-permute-done), channel_id=1, source_target_pairs={{1,0},{2,1},{3,2},{4,3},{5,4},{6,5},{7,6},{8,7},{9,8},{10,9},{11,1... | collective-permute-start | bytes 393224 | tf_op jit(solution)/shard_map/ppermute | solution.py:24
  211.8 10.3 %copy-start.3 = (f32[8,256]{1,0:T(8,128)S(1)}, f32[8,256]{1,0:T(8,128)}, u32[]{:S(2)}) copy-start(f32[8,256]{1,0:T(8,128)} %param.7) | copy-start | bytes 24580
  211.8 146.3 %all-to-all-start = ((f32[32,8,4096]{2,0,1:T(8,128)}), f32[32,8,4096]{2,0,1:T(8,128)}, u32[]{:S(2)}, u32[]{:S(2)}) async-start(f32[32,8,4096]{2,0,1:T(8,128)} %copy.16), calls=%async_computation | async-start | bytes 8388608 | tf_op jit(solution)/shard_map/all_to_all | solution.py:147
  221.3 136.8 %all-gather.3.cloned.1.call-start = ((), (), s32[]{:S(2)}) async-start(), calls=%async_computation.4 | async-start | bytes 1081344 | tf_op jit(solution)/shard_map/all_gather | solution.py:98
  222.0 198.1 %reduce-scatter.6.cloned.1.call-start = ((), (), s32[]{:S(2)}) async-start(), calls=%async_computation.5 | async-start | bytes 73728 | tf_op jit(solution)/shard_map/reduce_scatter | solution.py:127
  358.1 6.2 copy-start
  364.3 4.7 copy-start.4
  368.9 215.3 %reduce-scatter.8.cloned.1.call-start = ((), (), s32[]{:S(2)}) async-start(), calls=%async_computation.6 | async-start | bytes 1081344 | tf_op jit(solution)/shard_map/reduce_scatter | solution.py:156
  443.3 140.9 %copy-start.2 = (f32[64,128]{1,0:T(8,128)S(1)}, f32[64,128]{1,0:T(8,128)}, u32[]{:S(2)}) copy-start(f32[64,128]{1,0:T(8,128)} %param.6) | copy-start | bytes 98308
  447.0 266.4 %all-gather.5.cloned.1.call-start = ((), (), s32[]{:S(2)}) async-start(), calls=%async_computation.7 | async-start | bytes 1081344 | tf_op jit(solution)/shard_map/all_gather | solution.py:98
  585.7 191.1 %reduce-scatter.10.cloned.1.call-start = ((), (), s32[]{:S(2)}) async-start(), calls=%async_computation.8 | async-start | bytes 73728 | tf_op jit(solution)/shard_map/reduce_scatter | solution.py:127
  713.3 6.2 copy-start.1
Sparse Core Ops, SparseCore 0:
  223.8 134.2 all-gather.2
  369.0 51.0 reduce-scatter.5
  447.1 137.0 reduce-scatter.7
  586.3 126.9 all-gather.4
  724.2 52.4 reduce-scatter.9
where the time goes:
time: 793 us; the launch traced here: 785 us
  waiting for transfers between devices  267 us (34%)
  blocking collectives  255 us (32%)
  matrix products  86.6 us (11%)
  other arithmetic  63.4 us (8%)
  local copies, waits for them, and re-layouts  56.9 us (7%)
  loops' own time  27 us (3%)
  between operations  14.8 us (2%)
  starting transfers between devices  14.2 us (2%)
    all_gather x2, waiting for transfers between devices, gather_basis(): return lax.all_gather(own_columns, 'frames', axis=1, tiled=True)  155 us
    all_gather x2, blocking collectives, gather_activity(): return lax.all_gather(own_rows, 'freq', axis=0, tiled=True)  125 us
    psum x1, blocking collectives, on_device(): totals = lax.psum(totals, 'frames')  68.7 us
    reduce_scatter x1, waiting for transfers between devices, on_device(): lax.psum_scatter(numerator, 'frames', scatter_dimension=1, tiled=True)  68.4 us
    unnamed x2, blocking collectives  61.3 us
    reduce_scatter x2, waiting for transfers between devices, update_activity(): lax.psum_scatter(numerator, 'freq', scatter_dimension=0, tiled=True)  40.8 us
    unnamed x1, other arithmetic  34.1 us
    dot_general x8, matrix products, per_block(): jnp.einsum('oc,gjc->goj', second_section, twisted, precision=PRECISE, pre...  28.2 us
  transfers between devices with their start and end apart: 8, of which 6 were waited for; matrix products, arithmetic and copies ran while one was open for 5% of the time, Pallas kernels for 0%

commit v1 on v0

v1 whole, which is shorter than its diff:
```python
import math

import jax
import jax.numpy as jnp
import ml_dtypes
import numpy as np
from jax import lax
from jax.experimental import pallas as pl
from jax.experimental.pallas import tpu as pltpu
from jax.sharding import PartitionSpec as P

MESH = pl.DeviceIdType.MESH
F32 = jnp.float32
BF16 = jnp.bfloat16


def halves(table):
    high = table.astype(ml_dtypes.bfloat16)
    low = (table - high.astype(np.float64)).astype(ml_dtypes.bfloat16)
    return high, low


def build_tables():
    rows = np.arange(256)
    lanes = np.arange(128)
    m = (rows[:, None] * 128 + lanes[None, :]).astype(np.float64)
    window = (0.5 - 0.5 * np.cos(2 * math.pi / 65536 * m)).astype(np.float32)
    first = []
    twiddle = []
    for odd in (0, 1):
        k1 = 2 * np.arange(128) + odd
        angle = 2 * math.pi / 512 * (k1[:, None] * rows[None, :] % 512)
        real, imag = np.cos(angle), -np.sin(angle)
        if not odd:
            imag[0] = 1.0 - 2.0 * (rows % 2)
        first.append(np.concatenate([real, imag], 0))
        twiddle.append(2 * math.pi / 65536 * (k1[:, None] * lanes[None, :]))
    twiddle = np.concatenate(twiddle, 0)
    first = np.stack([np.stack(halves(part)) for part in first])
    second = []
    special = []
    lam = np.arange(128)
    z, x, rev, other = lam % 8, lam // 8 % 4, lam // 32 % 2, lam // 64
    for core in (0, 1):
        base = 8 * (2 * (z // 2) + (core ^ other)) + 4 * (z % 2) + x
        k2 = np.where(rev == 1, 127 - base, base)
        angle = 2 * math.pi / 128 * (lanes[:, None] * k2[None, :] % 128)
        cos, sin = np.cos(angle) / 32, np.sin(angle) / 32
        second.append(np.stack(halves(np.concatenate([np.concatenate([cos, -sin], 1), np.concatenate([sin, cos], 1)], 0))))
        angle = 2 * math.pi / 128 * (lanes[:, None] * (base + 0.5 * rev)[None, :])
        cos, sin = np.cos(angle) / 32, np.sin(angle) / 32
        keep, turn = (1 - rev)[None, :], rev[None, :]
        special.append(
            np.stack(
                halves(
                    np.concatenate(
                        [np.concatenate([cos * keep, -sin * keep], 1), np.concatenate([cos * turn, -sin * turn], 1)], 0
                    )
                )
            )
        )
    sigma = np.where(lanes < 64, 2 * lanes, 2 * (lanes - 64) + 1)
    perms = []
    for order in (sigma, (128 - sigma) % 128):
        perm = np.zeros((128, 128))
        perm[order, lanes] = 1.0
        perms += [perm, perm.T]
    perms = np.stack(perms).astype(ml_dtypes.bfloat16)
    return (
        window,
        np.cos(twiddle).astype(np.float32),
        np.sin(twiddle).astype(np.float32),
        first,
        np.stack(second),
        np.stack(special),
        perms,
    )


def split(value):
    high = value.astype(BF16)
    return high, (value - high.astype(F32)).astype(BF16)


def dot(a, b):
    return jnp.dot(a, b, preferred_element_type=F32)


def dot_t(a, b):
    return lax.dot_general(a, b, (((1,), (1,)), ((), ())), preferred_element_type=F32)


def moved(value, perm):
    high = value.astype(BF16)
    rest = value - high.astype(F32)
    middle = rest.astype(BF16)
    low = (rest - middle.astype(F32)).astype(BF16)
    return dot(high, perm) + dot(middle, perm) + dot(low, perm)


def doubled(value):
    high, low = split(value)
    lane = lax.broadcasted_iota(jnp.int32, value.shape, 1)
    both = jnp.where(lane < 64, high.astype(F32), low.astype(F32)).astype(BF16)
    return jnp.concatenate([both, both], 1)


def kernel(
    sig_hbm, templ, act, window, tcos, tsin, first, second, special, perms,
    out_act, out_templ,
    sigv, hg, ht, mag, zrow, mag0, sg, tsend, w, wn, num,
    r1a, r1b, r2a, r2b, q1a, q1b, q2a, q2b, rz,
    acc, sx, rx, sy, ry, tsx, trx, try_, trz, tsy, tsz, fin, fo,
    lsem, ssem, rsem,
):
    f = lax.axis_index("freq")
    t = lax.axis_index("frames")
    b = f % 2
    z_hi = f // 2
    z_lo = t // 16
    x = t // 4 % 4
    y = t % 4
    z = z_hi * 2 + z_lo
    partner = (f + 1 - 2 * b, t)

    def at_x(d):
        return (f, z_lo * 16 + (x + d) % 4 * 4 + y)

    def at_y(d):
        return (f, z_lo * 16 + x * 4 + (y + d) % 4)

    def at_z(d):
        other = (z + d) % 8
        return (other // 2 * 2 + b, other % 2 * 16 + x * 4 + y)

    def at_f(d):
        return ((f + d) % 8, t)

    def at_line(d):
        place = (t * 8 + f + d + 256) % 256
        return (place % 8, place // 8)

    greet = [partner] + [at_x(d) for d in (1, 2, 3)] + [at_y(d) for d in (1, 2, 3)]
    greet += [at_z(d) for d in range(1, 8)] + [at_f(d) for d in range(1, 8)] + [at_line(-1), at_line(1)]
    barrier = pltpu.get_barrier_semaphore()
    for device in greet:
        pl.semaphore_signal(barrier, inc=1, device_id=device, device_id_type=MESH)
    pl.semaphore_wait(barrier, len(greet))

    used = [0]

    def slot():
        used[0] += 1
        return used[0] - 1

    def remote(src, dst, index, device):
        return pltpu.make_async_remote_copy(
            src_ref=src, dst_ref=dst, send_sem=ssem.at[index], recv_sem=rsem.at[index],
            device_id=device, device_id_type=MESH,
        )

    loads = [
        pltpu.make_async_copy(sig_hbm.at[pl.ds(8 * i, 8)], sigv.at[pl.ds(8 * i, 8)], lsem.at[i]) for i in range(4)
    ]
    for load in loads:
        load.start()
    halo = remote(sig_hbm.at[0], sigv.at[32], slot(), at_line(-1))
    halo.start()
    h_copies = [remote(act, hg.at[f], slot(), at_f(d)) for d in range(1, 8)]
    for copy in h_copies:
        copy.start()
    hg[pl.ds(f, 1)] = act[...][None]

    flip = y // 2
    w[y, x, z] = moved(templ[...], perms[2 * flip])

    def gather_steps(buf):
        zc = [remote(buf.at[y, x, z], buf.at[y, x, z], slot(), at_z(d)) for d in range(1, 8)]
        lo, hi = pl.ds(0, 32), pl.ds(32, 32)

        def pair(region, right, left):
            return [remote(region, region, slot(), right), remote(region, region, slot(), left)]

        yl, yr, xl, xr = (y + 3) % 4, (y + 1) % 4, (x + 3) % 4, (x + 1) % 4
        a_own = buf.at[y, x, :, lo]
        b_own = buf.at[y, x, :, hi]
        p2s1 = pair(a_own, at_x(1), at_x(3)) + pair(b_own, at_y(1), at_y(3))

        def forward(to_right, right, to_left, left):
            return [remote(to_right, to_right, slot(), right), remote(to_left, to_left, slot(), left)]

        p2s2 = forward(buf.at[y, xl, pl.ds(0, 4), lo], at_x(1), buf.at[y, xr, pl.ds(4, 4), lo], at_x(3))
        p2s2 += forward(buf.at[yl, x, pl.ds(0, 4), hi], at_y(1), buf.at[yr, x, pl.ds(4, 4), hi], at_y(3))
        p3s1 = pair(buf.at[y, :, :, lo], at_y(1), at_y(3)) + pair(buf.at[:, x, :, hi], at_x(1), at_x(3))
        p3s2 = forward(buf.at[yl, pl.ds(0, 2), :, lo], at_y(1), buf.at[yr, pl.ds(2, 2), :, lo], at_y(3))
        p3s2 += forward(buf.at[pl.ds(0, 2), xl, :, hi], at_x(1), buf.at[pl.ds(2, 2), xr, :, hi], at_x(3))
        return [zc, p2s1, p2s2, p3s1, p3s2]

    def start(copies):
        for copy in copies:
            copy.start()

    def arrive(copies):
        for copy in copies:
            copy.wait_recv()

    def sent(copies):
        for copy in copies:
            copy.wait_send()

    w_steps = gather_steps(w)
    start(w_steps[0])
    s_slots = [slot() for _ in range(4)]

    def s_copy(group, index):
        return remote(tsend.at[group], sg.at[4 * b + group], index, partner)

    zrow[...] = jnp.zeros_like(zrow)

    def pair_step(group, p):
        n = group * 8 + 2 * p
        step = group * 4 + p
        for when, stage in ((1, 0), (3, 1), (5, 2), (12, 3)):
            @pl.when(step == when)
            def _(stage=stage):
                arrive(w_steps[stage])
                start(w_steps[stage + 1])

        win = window[...]
        h0, h1, h2 = sigv[n], sigv[n + 1], sigv[n + 2]
        a0, a1 = h0 * win, h1 * win
        b1, b2 = h1 - a1, h2 - h2 * win
        ev, ov = [], []
        for parity, block in ((0, jnp.concatenate([a0 + b1, a1 + b2], 1)), (1, jnp.concatenate([a0 - b1, a1 - b2], 1))):
            high, low = split(block)
            d_high, d_low = first[parity, 0], first[parity, 1]
            part = dot(d_high, high) + dot(d_high, low) + dot(d_low, high)
            (ev if parity == 0 else ov).append(part)
        pieces = []
        for frame in range(2):
            for parity, part in ((0, ev[0]), (1, ov[0])):
                real = part[:128, 128 * frame:128 * frame + 128]
                imag = part[128:, 128 * frame:128 * frame + 128]
                tc = tcos[128 * parity:128 * parity + 128, :]
                ts = tsin[128 * parity:128 * parity + 128, :]
                piece = jnp.concatenate([real * tc + imag * ts, imag * tc - real * ts], 1)
                if parity == 0:
                    zrow[pl.ds(2 * p + frame, 1), :] = piece[:1]
                pieces.append(piece)
        m_high, m_low = second[b, 0], second[b, 1]
        for frame in range(2):
            high, low = split(jnp.concatenate(pieces[2 * frame:2 * frame + 2], 0))
            out = dot(high, m_high) + dot(low, m_high) + dot(high, m_low)
            real, imag = out[:, :128], out[:, 128:]
            mag[2 * p + frame] = jnp.sqrt(real * real + imag * imag)

    lane = lax.broadcasted_iota(jnp.int32, (128, 128), 1)
    row = lax.broadcasted_iota(jnp.int32, (128, 128), 0)
    mirrored = lane // 32 % 2 == 1
    top = row == 0

    def turn(group, j):
        m = mag[j]
        low = jnp.concatenate([m[:64], m[128:192]], 0)
        high = jnp.concatenate([m[64:128], m[192:]], 0)
        extra = jnp.broadcast_to(mag0[pl.ds(j, 1), :], (128, 128))
        high_row = jnp.broadcast_to(high[:1], (128, 128))
        low = jnp.where(top, jnp.where(mirrored, high_row, extra), low)
        high = jnp.where(top & mirrored, extra, high)
        low, high = low.T, high.T
        for ref, index, off in ((sg, 4 * b + group, 0), (tsend, group, 64)):
            for value, place, part in ((low, 0, 0), (high, 1, 0), (high, 2, 1), (low, 3, 1)):
                ref[index, pl.ds(256 * place + j, 32, stride=8), :] = value[off + 32 * part:off + 32 * part + 32]

    def group_step(group, _):
        @pl.when(group == 0)
        def _():
            loads[0].wait()
            loads[1].wait()

        @pl.when(group == 1)
        def _():
            loads[2].wait()

        @pl.when(group == 2)
        def _():
            loads[3].wait()

        @pl.when(group == 3)
        def _():
            halo.wait_recv()
            sigv[32] = sigv[32] * jnp.where(t * 8 + f == 255, 0.0, 1.0)

        def body(p, _):
            pair_step(group, p)
            return 0

        lax.fori_loop(0, 4, body, 0)
        high, low = split(zrow[...])
        out = dot(high, special[b, 0]) + dot(low, special[b, 0]) + dot(high, special[b, 1])
        mag0[...] = jnp.sqrt(out[:, :128] * out[:, :128] + out[:, 128:] * out[:, 128:])

        def turn_body(j, _):
            turn(group, 2 * j)
            turn(group, 2 * j + 1)
            return 0

        lax.fori_loop(0, 4, turn_body, 0)
        for g in range(4):
            @pl.when(group == g)
            def _(g=g):
                s_copy(g, s_slots[g]).start()
        return 0

    lax.fori_loop(0, 4, group_step, 0)

    arrive(h_copies)
    rows64 = hg[...].reshape(64, 256)
    ht[...] = jnp.concatenate([rows64, rows64], 0).T
    h2 = ht[pl.ds(pl.multiple_of(64 * z_hi, 64), 64), :]
    arrive(w_steps[4])
    for g in range(4):
        s_copy(g, s_slots[g]).wait_recv()

    def frames_block(yy, xx):
        cols = []
        for k in range(8):
            place = pl.multiple_of(((yy * 4 + xx) * 8 + k) * 8, 8)
            cols.append(jnp.concatenate([sg[g, pl.ds(place, 8), :] for g in range(8)], 0))
        return jnp.concatenate(cols, 1)

    def ratio_of(buf, lhs, yy, xx):
        wide = jnp.concatenate([buf[yy, xx, k] for k in range(8)], 1)
        high, low = split(wide)
        approx = dot(lhs, jnp.concatenate([high, high, low, low], 0))
        return frames_block(yy, xx) / approx, high, low

    def gain_block(buf, lhs, yy, xx):
        ratio, high, low = ratio_of(buf, lhs, yy, xx)
        r_high, r_low = split(ratio)
        left = jnp.concatenate([r_high, r_low, jnp.ones((16, 1024), BF16)], 0)
        acc[...] += dot_t(left, jnp.concatenate([high, low], 0))

    def gain(stage, index):
        total = acc[...]
        part = jnp.concatenate([total[:64] + total[64:128], total[128:136]], 0)
        stage_send, stage_recv = stage
        stage_send[...] = part + pltpu.roll(part, 64, 1)
        copy = remote(stage_send, stage_recv, index, partner)
        copy.start()
        copy.wait_recv()
        both = stage_send[...] + stage_recv[...]
        return both[:64] / both[64:65], copy

    lhs1 = doubled(h2)
    acc[...] = jnp.zeros_like(acc)

    def first_body(i, _):
        gain_block(w, lhs1, i // 4, i % 4)
        return 0

    lax.fori_loop(0, 16, first_body, 0)
    gain1, mid_copy = gain((sx, rx), slot())
    mid = h2 * gain1
    mid_lhs = doubled(mid)
    mid_t = jnp.concatenate([mid, mid], 0).T
    mid_left = doubled(mid_t[:64])

    tsx[...] = jnp.broadcast_to(jnp.sum(mid, axis=0, keepdims=True), (8, 128))
    tx_copies = [remote(tsx, trx.at[d - 1], slot(), at_x(d)) for d in (1, 2, 3)]
    start(tx_copies)

    def num_block(yy, xx):
        ratio, _, _ = ratio_of(w, mid_lhs, yy, xx)
        high, low = split(ratio)
        out = dot(mid_left, jnp.concatenate([high, high, low, low], 0))
        for k in range(8):
            num[yy, xx, k] = out[:, 128 * k:128 * k + 128]

    lo, hi = pl.ds(0, 32), pl.ds(32, 32)
    yl, yr, yo = (y + 3) % 4, (y + 1) % 4, (y + 2) % 4
    xl, xr, xo = (x + 3) % 4, (x + 1) % 4, (x + 2) % 4

    def num_run(blocks):
        def body(i, _):
            dy, dx = blocks(i)
            num_block((y + dy) % 4, (x + dx) % 4)
            return 0
        return body

    def run(count, blocks):
        lax.fori_loop(0, count, num_run(blocks), 0)

    run(4, lambda i: (2, i))
    a1 = [
        remote(num.at[yo, pl.ds(0, 2), :, lo], r1a.at[0], slot(), at_y(1)),
        remote(num.at[yo, pl.ds(2, 2), :, lo], r1a.at[1], slot(), at_y(3)),
    ]
    start(a1)
    run(3, lambda i: ((i + 3) % 4, 2))
    b1 = [
        remote(num.at[pl.ds(0, 2), xo, :, hi], r1b.at[0], slot(), at_x(1)),
        remote(num.at[pl.ds(2, 2), xo, :, hi], r1b.at[1], slot(), at_x(3)),
    ]
    start(b1)
    run(3, lambda i: (1, (i + 3) % 4))
    run(3, lambda i: (3, (i + 3) % 4))

    def add_loop(count, fn):
        def body(i, _):
            fn(i)
            return 0
        lax.fori_loop(0, count, body, 0)

    arrive(a1)

    def add_a1(i):
        num[yr, i // 8, i % 8, lo] += r1a[0, i // 8, i % 8]
        num[yl, 2 + i // 8, i % 8, lo] += r1a[1, i // 8, i % 8]

    add_loop(16, add_a1)
    a2 = [
        remote(num.at[yr, :, :, lo], r2a.at[0], slot(), at_y(1)),
        remote(num.at[yl, :, :, lo], r2a.at[1], slot(), at_y(3)),
    ]
    start(a2)
    run(2, lambda i: (0, 1 + 2 * i))
    arrive(b1)

    def add_b1(i):
        num[i // 8, xr, i % 8, hi] += r1b[0, i // 8, i % 8]
        num[2 + i // 8, xl, i % 8, hi] += r1b[1, i // 8, i % 8]

    add_loop(16, add_b1)
    b2 = [
        remote(num.at[:, xr, :, hi], r2b.at[0], slot(), at_x(1)),
        remote(num.at[:, xl, :, hi], r2b.at[1], slot(), at_x(3)),
    ]
    start(b2)
    run(1, lambda i: (0, 0))

    arrive(tx_copies)
    tsy[...] = tsx[...] + trx[0] + trx[1] + trx[2]
    ty_copies = [remote(tsy, try_.at[d - 1], slot(), at_y(d)) for d in (1, 2, 3)]
    start(ty_copies)

    arrive(a2)

    def add_a2(i):
        num[y, i // 8, i % 8, lo] += r2a[0, i // 8, i % 8] + r2a[1, i // 8, i % 8]

    add_loop(32, add_a2)
    c1 = [
        remote(num.at[y, xo, pl.ds(0, 4), lo], q1a.at[0], slot(), at_x(1)),
        remote(num.at[y, xo, pl.ds(4, 4), lo], q1a.at[1], slot(), at_x(3)),
    ]
    start(c1)
    arrive(b2)

    def add_b2(i):
        num[i // 8, x, i % 8, hi] += r2b[0, i // 8, i % 8] + r2b[1, i // 8, i % 8]

    add_loop(32, add_b2)
    d1 = [
        remote(num.at[yo, x, pl.ds(0, 4), hi], q1b.at[0], slot(), at_y(1)),
        remote(num.at[yo, x, pl.ds(4, 4), hi], q1b.at[1], slot(), at_y(3)),
    ]
    start(d1)
    arrive(c1)

    def add_c1(i):
        num[y, xr, i, lo] += q1a[0, i]
        num[y, xl, 4 + i, lo] += q1a[1, i]

    add_loop(4, add_c1)
    c2 = [
        remote(num.at[y, xr, :, lo], q2a.at[0], slot(), at_x(1)),
        remote(num.at[y, xl, :, lo], q2a.at[1], slot(), at_x(3)),
    ]
    start(c2)
    arrive(d1)

    def add_d1(i):
        num[yr, x, i, hi] += q1b[0, i]
        num[yl, x, 4 + i, hi] += q1b[1, i]

    add_loop(4, add_d1)
    d2 = [
        remote(num.at[yr, x, :, hi], q2b.at[0], slot(), at_y(1)),
        remote(num.at[yl, x, :, hi], q2b.at[1], slot(), at_y(3)),
    ]
    start(d2)

    arrive(ty_copies)
    tsz[...] = tsy[...] + try_[0] + try_[1] + try_[2]
    tz_copies = [remote(tsz, trz.at[d - 1], slot(), at_z(d)) for d in range(1, 8)]
    start(tz_copies)

    arrive(c2)
    arrive(d2)

    def add_cd2(i):
        num[y, x, i, lo] += q2a[0, i] + q2a[1, i]
        num[y, x, i, hi] += q2b[0, i] + q2b[1, i]

    add_loop(8, add_cd2)
    z_copies = [remote(num.at[y, x, (z + d) % 8], rz.at[d - 1], slot(), at_z(d)) for d in range(1, 8)]
    start(z_copies)
    arrive(tz_copies)
    totals = tsz[...]
    for d in range(7):
        totals = totals + trz[d]
    totals = jnp.broadcast_to(totals[:1], (128, 128)).T[:64]
    arrive(z_copies)
    whole = num[y, x, z]
    for d in range(7):
        whole = whole + rz[d]
    wn[y, x, z] = w[y, x, z] * (whole / totals)

    n_steps = gather_steps(wn)
    start(n_steps[0])
    out_templ[...] = moved(wn[y, x, z], perms[2 * flip + 1])
    acc[...] = jnp.zeros_like(acc)
    for stage in range(3):
        arrive(n_steps[stage])
        start(n_steps[stage + 1])
    arrive(n_steps[3])
    start(n_steps[4])

    def near_body(i, _):
        gain_block(wn, mid_lhs, (y + 3 + i // 3) % 4, (x + 3 + i % 3) % 4)
        return 0

    lax.fori_loop(0, 9, near_body, 0)
    arrive(n_steps[4])

    def far_body(i, _):
        gain_block(wn, mid_lhs, (y + 2) % 4, i)
        return 0

    lax.fori_loop(0, 4, far_body, 0)

    def side_body(i, _):
        gain_block(wn, mid_lhs, (y + 3 + i) % 4, (x + 2) % 4)
        return 0

    lax.fori_loop(0, 3, side_body, 0)
    gain2, last_copy = gain((sy, ry), slot())
    final = mid * gain2
    fin[...] = jnp.concatenate([final, final], 0).T
    f_copies = []
    for d in range(1, 4):
        other = (z_hi + d) % 4 * 2 + b
        rows = pl.ds(pl.multiple_of(8 * other, 8), 8)
        f_copies.append(remote(fin.at[rows], fo.at[z_hi], slot(), (other, t)))
    start(f_copies)
    fo[pl.ds(z_hi, 1)] = fin[pl.ds(pl.multiple_of(8 * f, 8), 8), :][None]
    arrive(f_copies)
    near = lax.broadcasted_iota(jnp.int32, (8, 128), 1) < 64
    out_act[:, :128] = jnp.where(near, fo[0], fo[1])
    out_act[:, 128:] = jnp.where(near, fo[2], fo[3])

    sent([halo] + h_copies)
    for stage in w_steps + n_steps:
        sent(stage)
    for g in range(4):
        s_copy(g, s_slots[g]).wait_send()
    sent([mid_copy, last_copy] + tx_copies + ty_copies + tz_copies)
    sent(a1 + b1 + a2 + b2 + c1 + d1 + c2 + d2 + z_copies + f_copies)


COPIES = 120


def on_device(signal, templates, activations):
    tables = build_tables()
    vmem = pl.BlockSpec(memory_space=pltpu.VMEM)
    f32 = lambda *shape: pltpu.VMEM(shape, F32)
    return pl.pallas_call(
        kernel,
        out_shape=(jax.ShapeDtypeStruct((8, 256), F32), jax.ShapeDtypeStruct((64, 128), F32)),
        in_specs=[pl.BlockSpec(memory_space=pl.ANY)] + [vmem] * 9,
        out_specs=(vmem, vmem),
        scratch_shapes=[
            f32(33, 256, 128),
            f32(8, 8, 256),
            f32(256, 128),
            f32(8, 256, 128),
            f32(16, 256),
            f32(16, 128),
            f32(8, 1024, 128),
            f32(4, 1024, 128),
            f32(4, 4, 8, 64, 128),
            f32(4, 4, 8, 64, 128),
            f32(4, 4, 8, 64, 128),
            f32(2, 2, 8, 32, 128),
            f32(2, 2, 8, 32, 128),
            f32(2, 4, 8, 32, 128),
            f32(2, 4, 8, 32, 128),
            f32(2, 4, 32, 128),
            f32(2, 4, 32, 128),
            f32(2, 8, 32, 128),
            f32(2, 8, 32, 128),
            f32(7, 64, 128),
            f32(144, 128),
            f32(72, 128), f32(72, 128), f32(72, 128), f32(72, 128),
            f32(8, 128),
            f32(3, 8, 128), f32(3, 8, 128), f32(7, 8, 128),
            f32(8, 128), f32(8, 128),
            f32(128, 128),
            f32(4, 8, 128),
            pltpu.SemaphoreType.DMA((4,)),
            pltpu.SemaphoreType.DMA((COPIES,)),
            pltpu.SemaphoreType.DMA((COPIES,)),
        ],
        compiler_params=pltpu.CompilerParams(
            collective_id=0, has_side_effects=True, vmem_limit_bytes=60 * 1024 * 1024
        ),
    )(signal.reshape(32, 256, 128), templates, activations, *tables)


def solution(mesh):
    return jax.shard_map(
        on_device,
        mesh=mesh,
        in_specs=(P("frames", "freq", None), P(None, ("freq", "frames")), P("freq", "frames")),
        out_specs=(P("freq", "frames"), P(None, ("freq", "frames"))),
        check_vma=False,
    )
```

time: 793 us -> 150 us (0.19); the launches traced: 785 us -> 150 us
  waiting for transfers between devices: 267 us -> 0 us
  blocking collectives: 255 us -> 0 us
  Pallas kernels: 0 us -> 147 us
  matrix products: 86.6 us -> 0 us
  other arithmetic: 63.4 us -> 0 us
  local copies, waits for them, and re-layouts: 56.9 us -> 2.67 us
  loops' own time: 27 us -> 0 us
  starting transfers between devices: 14.2 us -> 0 us
  between operations: 14.8 us -> 0.64 us
    all_gather x2 -> x0, waiting for transfers between devices: 155 us -> none  [gather_basis(): return lax.all_gather(own_columns, 'frames', axis=1, tiled=True)]
    pallas_call x0 -> x1, Pallas kernels: none -> 147 us  [on_device(): pl.pallas_call(kernel, out_shape=(jax.ShapeDtypeStruct((8, 256), F32), ja...]
    all_gather x2 -> x0, blocking collectives: 125 us -> none  [gather_activity(): return lax.all_gather(own_rows, 'freq', axis=0, tiled=True)]
    reduce_scatter x3 -> x0, waiting for transfers between devices: 109 us -> none  [the longest x1 68.4 us: on_device(): lax.psum_scatter(numerator, 'frames', scatter_dimension=1, tiled=True)]
    dot_general x22 -> x0, matrix products: 86.6 us -> none  [the longest x8 28.2 us: per_block(): jnp.einsum('oc,gjc->goj', second_section, twisted, precision=PRECISE, pre...]
    psum x1 -> x0, blocking collectives: 68.7 us -> none  [on_device(): totals = lax.psum(totals, 'frames')]
    unnamed x2 -> x0, blocking collectives: 61.3 us -> none
    unnamed x1 -> x0, other arithmetic: 34.1 us -> none
  transfers between devices with their start and end apart: 8 -> 0, of which waited for: 6 -> 0; matrix products, arithmetic and copies ran while one was open for 5% -> 0% of each run, Pallas kernels for 0% -> 0%
where the time goes in v1:
time: 150 us
  Pallas kernels  147 us (98%)
  local copies, waits for them, and re-layouts  2.67 us (2%)
    pallas_call x1, Pallas kernels, on_device(): pl.pallas_call(kernel, out_shape=(jax.ShapeDtypeStruct((8, 256), F32), ja...  147 us

profile of v1, /device:TPU:1, one launch (start us, length us, event | category | flops | bytes accessed | tf_op | source)
XLA Modules:
  0.0 149.9 jit_solution(16821573590790009151)
XLA Ops:
  0.6 146.6 %shard_map.113 = (f32[8,256]{1,0:T(8,128)}, f32[64,128]{1,0:T(8,128)}) custom-call(f32[32,256,128]{2,1,0:T(8,128)} %bitcast.1, f32[64,128]{1,0:T(8,128)} %templ.1, f32[8,256]{1,0:T(8,128)} %act.1, f32[256,128]{1,0:T(8,128)} %constant.14.clone.window, f32[256,128]{1,0:T(8,128)} %constant.15.clone.tcos, f32[256,128]{1,0:T(8,128)} %constant.16.clone.tsin, ...), custom_call_target="tpu_custom_call" | custom-call | tf_op jit(solution)/shard_map/pallas_call | solution.py:579
  147.2 1.3 copy.14
  148.5 1.4 copy.15

commit v2 on v1

--- a/solution.py
+++ b/solution.py
@@ -109,7 +109,7 @@
     sig_hbm, templ, act, window, tcos, tsin, first, second, special, perms,
     out_act, out_templ,
     sigv, hg, ht, mag, zrow, mag0, sg, tsend, w, wn, num,
-    r1a, r1b, r2a, r2b, q1a, q1b, q2a, q2b, rz,
+    ha1, ha2, hb1, hb2, ma1, ma2, mb1, mb2, c1, c2, c3, c4, cyb, cxb, rz,
     acc, sx, rx, sy, ry, tsx, trx, try_, trz, tsy, tsz, fin, fo,
     lsem, ssem, rsem,
 ):
@@ -174,27 +174,94 @@
     flip = y // 2
     w[y, x, z] = moved(templ[...], perms[2 * flip])
 
-    def gather_steps(buf):
-        zc = [remote(buf.at[y, x, z], buf.at[y, x, z], slot(), at_z(d)) for d in range(1, 8)]
-        lo, hi = pl.ds(0, 32), pl.ds(32, 32)
-
-        def pair(region, right, left):
-            return [remote(region, region, slot(), right), remote(region, region, slot(), left)]
-
-        yl, yr, xl, xr = (y + 3) % 4, (y + 1) % 4, (x + 3) % 4, (x + 1) % 4
-        a_own = buf.at[y, x, :, lo]
-        b_own = buf.at[y, x, :, hi]
-        p2s1 = pair(a_own, at_x(1), at_x(3)) + pair(b_own, at_y(1), at_y(3))
-
-        def forward(to_right, right, to_left, left):
-            return [remote(to_right, to_right, slot(), right), remote(to_left, to_left, slot(), left)]
-
-        p2s2 = forward(buf.at[y, xl, pl.ds(0, 4), lo], at_x(1), buf.at[y, xr, pl.ds(4, 4), lo], at_x(3))
-        p2s2 += forward(buf.at[yl, x, pl.ds(0, 4), hi], at_y(1), buf.at[yr, x, pl.ds(4, 4), hi], at_y(3))
-        p3s1 = pair(buf.at[y, :, :, lo], at_y(1), at_y(3)) + pair(buf.at[:, x, :, hi], at_x(1), at_x(3))
-        p3s2 = forward(buf.at[yl, pl.ds(0, 2), :, lo], at_y(1), buf.at[yr, pl.ds(2, 2), :, lo], at_y(3))
-        p3s2 += forward(buf.at[pl.ds(0, 2), xl, :, hi], at_x(1), buf.at[pl.ds(2, 2), xr, :, hi], at_x(3))
-        return [zc, p2s1, p2s2, p3s1, p3s2]
+    lo, hi, low_rows = pl.ds(0, 24), pl.ds(24, 24), pl.ds(0, 48)
+    end = pl.ds(48, 16)
+    half = (pl.ds(0, 2), pl.ds(2, 2))
+    quad = (pl.ds(0, 4), pl.ds(4, 4))
+    every = slice(None)
+    yl, yr, yo = (y + 3) % 4, (y + 1) % 4, (y + 2) % 4
+    xl, xr, xo = (x + 3) % 4, (x + 1) % 4, (x + 2) % 4
+
+    def same(region, device):
+        return remote(region, region, slot(), device)
+
+    class Gather:
+        def __init__(self, buf):
+            self.zc = [same(buf.at[y, x, z, low_rows], at_z(d)) for d in range(1, 8)]
+            self.cx = [same(buf.at[y, x, z, end], at_x(d)) for d in (1, 2, 3)]
+            self.cy = [same(buf.at[y, every, z, end], at_y(d)) for d in (1, 2, 3)]
+            self.cz = []
+            for k in range(4):
+                right, left = (z + 8 - k) % 8, (z + k) % 8
+                parts = ((0, 1), (1, 0)) if k < 3 else ((0,), (1,))
+                ring = []
+                for i in range(len(parts[0])):
+                    ring.append(same(buf.at[half[parts[0][i]], every, right, end], at_z(1)))
+                    ring.append(same(buf.at[half[parts[1][i]], every, left, end], at_z(7)))
+                self.cz.append(ring)
+            a_own, b_own = buf.at[y, x, every, lo], buf.at[y, x, every, hi]
+            self.m1 = [same(a_own, at_x(1)), same(a_own, at_x(3)), same(b_own, at_y(1)), same(b_own, at_y(3))]
+            self.m2 = [
+                same(buf.at[y, xl, quad[0], lo], at_x(1)), same(buf.at[y, xr, quad[1], lo], at_x(3)),
+                same(buf.at[yl, x, quad[0], hi], at_y(1)), same(buf.at[yr, x, quad[1], hi], at_y(3)),
+            ]
+
+            def heavy(first_half):
+                right, left = (0, 1) if first_half else (1, 0)
+                return [
+                    same(buf.at[y, half[right], every, lo], at_y(1)), same(buf.at[y, half[left], every, lo], at_y(3)),
+                    same(buf.at[half[right], x, every, hi], at_x(1)), same(buf.at[half[left], x, every, hi], at_x(3)),
+                ]
+
+            self.h1, self.h1b = heavy(True), heavy(False)
+            self.h2 = [
+                same(buf.at[yl, half[0], every, lo], at_y(1)), same(buf.at[yr, half[1], every, lo], at_y(3)),
+                same(buf.at[half[0], xl, every, hi], at_x(1)), same(buf.at[half[1], xr, every, hi], at_x(3)),
+            ]
+
+        def event(self, k):
+            if k == 0:
+                start(self.cx)
+                start(self.zc)
+            elif k == 1:
+                arrive(self.cx)
+                start(self.cy)
+            elif k == 2:
+                arrive(self.zc)
+                start(self.m1)
+            elif k == 3:
+                arrive(self.cy)
+                start(self.cz[0])
+            elif k == 4:
+                arrive(self.m1)
+                start(self.m2)
+            elif k == 5:
+                self.ring(1)
+            elif k == 6:
+                arrive(self.m2)
+                start(self.h1)
+                start(self.h1b)
+            elif k == 7:
+                self.ring(2)
+            elif k == 8:
+                arrive(self.h1)
+                start(self.h2)
+            elif k == 9:
+                self.ring(3)
+            elif k == 10:
+                arrive(self.cz[3])
+                arrive(self.h1b)
+            else:
+                arrive(self.h2)
+
+        def ring(self, k):
+            for i in range(0, 4, 2):
+                arrive(self.cz[k - 1][i:i + 2])
+                start(self.cz[k][i:i + 2])
+
+        def all_sent(self):
+            for copies in [self.zc, self.cx, self.cy] + self.cz + [self.m1, self.m2, self.h1, self.h1b, self.h2]:
+                sent(copies)
 
     def start(copies):
         for copy in copies:
@@ -208,8 +275,8 @@
         for copy in copies:
             copy.wait_send()
 
-    w_steps = gather_steps(w)
-    start(w_steps[0])
+    w_gather = Gather(w)
+    w_gather.event(0)
     s_slots = [slot() for _ in range(4)]
 
     def s_copy(group, index):
@@ -220,11 +287,10 @@
     def pair_step(group, p):
         n = group * 8 + 2 * p
         step = group * 4 + p
-        for when, stage in ((1, 0), (3, 1), (5, 2), (12, 3)):
+        for when, event in ((3, 1), (6, 2), (7, 3), (10, 4), (12, 5), (14, 6)):
             @pl.when(step == when)
-            def _(stage=stage):
-                arrive(w_steps[stage])
-                start(w_steps[stage + 1])
+            def _(event=event):
+                w_gather.event(event)
 
         win = window[...]
         h0, h1, h2 = sigv[n], sigv[n + 1], sigv[n + 2]
@@ -318,7 +384,6 @@
     rows64 = hg[...].reshape(64, 256)
     ht[...] = jnp.concatenate([rows64, rows64], 0).T
     h2 = ht[pl.ds(pl.multiple_of(64 * z_hi, 64), 64), :]
-    arrive(w_steps[4])
     for g in range(4):
         s_copy(g, s_slots[g]).wait_recv()
 
@@ -355,11 +420,28 @@
     lhs1 = doubled(h2)
     acc[...] = jnp.zeros_like(acc)
 
-    def first_body(i, _):
-        gain_block(w, lhs1, i // 4, i % 4)
-        return 0
-
-    lax.fori_loop(0, 16, first_body, 0)
+    def gain_all(buf, lhs, gather):
+        def near_body(i, _):
+            gain_block(buf, lhs, (y + 3 + i // 3) % 4, (x + 3 + i % 3) % 4)
+            return 0
+
+        def far_body(i, _):
+            gain_block(buf, lhs, (y + 2) % 4, i)
+            return 0
+
+        def side_body(i, _):
+            gain_block(buf, lhs, (y + 3 + i) % 4, (x + 2) % 4)
+            return 0
+
+        gather.event(10)
+        lax.fori_loop(0, 9, near_body, 0)
+        gather.event(11)
+        lax.fori_loop(0, 4, far_body, 0)
+        lax.fori_loop(0, 3, side_body, 0)
+
+    for event in (7, 8, 9):
+        w_gather.event(event)
+    gain_all(w, lhs1, w_gather)
     gain1, mid_copy = gain((sx, rx), slot())
     mid = h2 * gain1
     mid_lhs = doubled(mid)
@@ -377,10 +459,6 @@
         for k in range(8):
             num[yy, xx, k] = out[:, 128 * k:128 * k + 128]
 
-    lo, hi = pl.ds(0, 32), pl.ds(32, 32)
-    yl, yr, yo = (y + 3) % 4, (y + 1) % 4, (y + 2) % 4
-    xl, xr, xo = (x + 3) % 4, (x + 1) % 4, (x + 2) % 4
-
     def num_run(blocks):
         def body(i, _):
             dy, dx = blocks(i)
@@ -391,160 +469,151 @@
     def run(count, blocks):
         lax.fori_loop(0, count, num_run(blocks), 0)
 
+    class Reduce4:
+        def __init__(self, get, once, twice, places, right, left):
+            own, right_place, left_place, far = places
+            self.get, self.once, self.twice, self.places = get, once, twice, places
+
+            def to(buf, side, part):
+                return buf.at[side] if part is None else buf.at[side, part]
+
+            self.first = [
+                remote(get(far, 0), once.at[0], slot(), right), remote(get(far, 1), once.at[1], slot(), left),
+            ]
+            size = once.shape[1]
+            parts = (pl.ds(0, size), pl.ds(size, size))
+            self.early = [
+                remote(get(right_place, 1), to(twice, 0, parts[1]), slot(), right),
+                remote(get(left_place, 0), to(twice, 1, parts[0]), slot(), left),
+            ]
+            self.late = [
+                remote(get(right_place, 0), to(twice, 0, parts[0]), slot(), right),
+                remote(get(left_place, 1), to(twice, 1, parts[1]), slot(), left),
+            ]
+
+        def pass_on(self):
+            own, right_place, left_place, far = self.places
+            arrive(self.first)
+            target = self.get(right_place, 0)
+            target[...] = target[...] + self.once[0]
+            target = self.get(left_place, 1)
+            target[...] = target[...] + self.once[1]
+            start(self.late)
+
+        def finish(self):
+            arrive(self.early)
+            arrive(self.late)
+            target = self.get(self.places[0], None)
+            target[...] = target[...] + (self.twice[0] + self.twice[1])
+
+        def all_sent(self):
+            sent(self.first + self.early + self.late)
+
+    def pick(parts, part):
+        return every if part is None else parts[part]
+
+    y_places, x_places = (y, yr, yl, yo), (x, xr, xl, xo)
+    ra = Reduce4(lambda i, p: num.at[i, pick(half, p), every, lo], ha1, ha2, y_places, at_y(1), at_y(3))
+    rb = Reduce4(lambda i, p: num.at[pick(half, p), i, every, hi], hb1, hb2, x_places, at_x(1), at_x(3))
+    na = Reduce4(lambda i, p: num.at[y, i, pick(quad, p), lo], ma1, ma2, x_places, at_x(1), at_x(3))
+    nb = Reduce4(lambda i, p: num.at[i, x, pick(quad, p), hi], mb1, mb2, y_places, at_y(1), at_y(3))
+
     run(4, lambda i: (2, i))
-    a1 = [
-        remote(num.at[yo, pl.ds(0, 2), :, lo], r1a.at[0], slot(), at_y(1)),
-        remote(num.at[yo, pl.ds(2, 2), :, lo], r1a.at[1], slot(), at_y(3)),
-    ]
-    start(a1)
+    start(ra.first)
     run(3, lambda i: ((i + 3) % 4, 2))
-    b1 = [
-        remote(num.at[pl.ds(0, 2), xo, :, hi], r1b.at[0], slot(), at_x(1)),
-        remote(num.at[pl.ds(2, 2), xo, :, hi], r1b.at[1], slot(), at_x(3)),
-    ]
-    start(b1)
+    start(rb.first)
     run(3, lambda i: (1, (i + 3) % 4))
     run(3, lambda i: (3, (i + 3) % 4))
-
-    def add_loop(count, fn):
-        def body(i, _):
-            fn(i)
-            return 0
-        lax.fori_loop(0, count, body, 0)
-
-    arrive(a1)
-
-    def add_a1(i):
-        num[yr, i // 8, i % 8, lo] += r1a[0, i // 8, i % 8]
-        num[yl, 2 + i // 8, i % 8, lo] += r1a[1, i // 8, i % 8]
-
-    add_loop(16, add_a1)
-    a2 = [
-        remote(num.at[yr, :, :, lo], r2a.at[0], slot(), at_y(1)),
-        remote(num.at[yl, :, :, lo], r2a.at[1], slot(), at_y(3)),
+    start(ra.early)
+    run(2, lambda i: (0, 1 + 2 * i))
+    start(rb.early)
+    run(1, lambda i: (0, 0))
+
+    def zz(d):
+        return (z + 8 + d) % 8
+
+    ring1 = [
+        remote(num.at[half[0], every, zz(4), end], c1.at[0], slot(), at_z(1)),
+        remote(num.at[half[1], every, zz(4), end], c1.at[1], slot(), at_z(7)),
     ]
-    start(a2)
-    run(2, lambda i: (0, 1 + 2 * i))
-    arrive(b1)
-
-    def add_b1(i):
-        num[i // 8, xr, i % 8, hi] += r1b[0, i // 8, i % 8]
-        num[2 + i // 8, xl, i % 8, hi] += r1b[1, i // 8, i % 8]
-
-    add_loop(16, add_b1)
-    b2 = [
-        remote(num.at[:, xr, :, hi], r2b.at[0], slot(), at_x(1)),
-        remote(num.at[:, xl, :, hi], r2b.at[1], slot(), at_x(3)),
-    ]
-    start(b2)
-    run(1, lambda i: (0, 0))
+    start(ring1)
+
+    def ring_send(buf, d):
+        copies = [
+            remote(num.at[every, every, zz(d), end], buf.at[0], slot(), at_z(1)),
+            remote(num.at[every, every, zz(-d), end], buf.at[1], slot(), at_z(7)),
+        ]
+        start(copies)
+        return copies
+
+    def ring_add(buf, d):
+        for side, place in ((0, zz(d)), (1, zz(-d))):
+            target = num.at[every, every, place, end]
+            target[...] = target[...] + buf[side]
 
     arrive(tx_copies)
     tsy[...] = tsx[...] + trx[0] + trx[1] + trx[2]
     ty_copies = [remote(tsy, try_.at[d - 1], slot(), at_y(d)) for d in (1, 2, 3)]
     start(ty_copies)
-
-    arrive(a2)
-
-    def add_a2(i):
-        num[y, i // 8, i % 8, lo] += r2a[0, i // 8, i % 8] + r2a[1, i // 8, i % 8]
-
-    add_loop(32, add_a2)
-    c1 = [
-        remote(num.at[y, xo, pl.ds(0, 4), lo], q1a.at[0], slot(), at_x(1)),
-        remote(num.at[y, xo, pl.ds(4, 4), lo], q1a.at[1], slot(), at_x(3)),
-    ]
-    start(c1)
-    arrive(b2)
-
-    def add_b2(i):
-        num[i // 8, x, i % 8, hi] += r2b[0, i // 8, i % 8] + r2b[1, i // 8, i % 8]
-
-    add_loop(32, add_b2)
-    d1 = [
-        remote(num.at[yo, x, pl.ds(0, 4), hi], q1b.at[0], slot(), at_y(1)),
-        remote(num.at[yo, x, pl.ds(4, 4), hi], q1b.at[1], slot(), at_y(3)),
-    ]
-    start(d1)
-    arrive(c1)
-
-    def add_c1(i):
-        num[y, xr, i, lo] += q1a[0, i]
-        num[y, xl, 4 + i, lo] += q1a[1, i]
-
-    add_loop(4, add_c1)
-    c2 = [
-        remote(num.at[y, xr, :, lo], q2a.at[0], slot(), at_x(1)),
-        remote(num.at[y, xl, :, lo], q2a.at[1], slot(), at_x(3)),
-    ]
-    start(c2)
-    arrive(d1)
-
-    def add_d1(i):
-        num[yr, x, i, hi] += q1b[0, i]
-        num[yl, x, 4 + i, hi] += q1b[1, i]
-
-    add_loop(4, add_d1)
-    d2 = [
-        remote(num.at[yr, x, :, hi], q2b.at[0], slot(), at_y(1)),
-        remote(num.at[yl, x, :, hi], q2b.at[1], slot(), at_y(3)),
-    ]
-    start(d2)
-
+    arrive(ring1)
+    for side, place in ((0, zz(3)), (1, zz(-3))):
+        target = num.at[half[side], every, place, end]
+        target[...] = target[...] + c1[side]
+    ring2 = ring_send(c2, 3)
+    ra.pass_on()
+    rb.pass_on()
     arrive(ty_copies)
     tsz[...] = tsy[...] + try_[0] + try_[1] + try_[2]
     tz_copies = [remote(tsz, trz.at[d - 1], slot(), at_z(d)) for d in range(1, 8)]
     start(tz_copies)
-
-    arrive(c2)
-    arrive(d2)
-
-    def add_cd2(i):
-        num[y, x, i, lo] += q2a[0, i] + q2a[1, i]
-        num[y, x, i, hi] += q2b[0, i] + q2b[1, i]
-
-    add_loop(8, add_cd2)
-    z_copies = [remote(num.at[y, x, (z + d) % 8], rz.at[d - 1], slot(), at_z(d)) for d in range(1, 8)]
-    start(z_copies)
+    arrive(ring2)
+    ring_add(c2, 2)
+    ring3 = ring_send(c3, 2)
+    arrive(ring3)
+    ring_add(c3, 1)
+    ring4 = ring_send(c4, 1)
+    ra.finish()
+    start(na.first + na.early)
+    rb.finish()
+    start(nb.first + nb.early)
+    arrive(ring4)
+    target = num.at[every, every, z, end]
+    target[...] = target[...] + (c4[0] + c4[1])
+    cy_copies = [remote(num.at[(y + d) % 4, every, z, end], cyb.at[d - 1], slot(), at_y(d)) for d in (1, 2, 3)]
+    start(cy_copies)
+    na.pass_on()
+    nb.pass_on()
     arrive(tz_copies)
     totals = tsz[...]
     for d in range(7):
         totals = totals + trz[d]
     totals = jnp.broadcast_to(totals[:1], (128, 128)).T[:64]
+    arrive(cy_copies)
+    target = num.at[y, every, z, end]
+    target[...] = target[...] + (cyb[0] + cyb[1] + cyb[2])
+    cx_copies = [remote(num.at[y, (x + d) % 4, z, end], cxb.at[d - 1], slot(), at_x(d)) for d in (1, 2, 3)]
+    start(cx_copies)
+    na.finish()
+    nb.finish()
+    z_copies = [remote(num.at[y, x, zz(d), low_rows], rz.at[d - 1], slot(), at_z(d)) for d in range(1, 8)]
+    start(z_copies)
+    arrive(cx_copies)
+    whole = num[y, x, z, end] + (cxb[0] + cxb[1] + cxb[2])
+    wn[y, x, z, end] = w[y, x, z, end] * (whole / totals[48:])
+    n_gather = Gather(wn)
+    start(n_gather.cx)
     arrive(z_copies)
-    whole = num[y, x, z]
+    whole = num[y, x, z, low_rows]
     for d in range(7):
         whole = whole + rz[d]
-    wn[y, x, z] = w[y, x, z] * (whole / totals)
-
-    n_steps = gather_steps(wn)
-    start(n_steps[0])
+    wn[y, x, z, low_rows] = w[y, x, z, low_rows] * (whole / totals[:48])
+    start(n_gather.zc)
+
     out_templ[...] = moved(wn[y, x, z], perms[2 * flip + 1])
     acc[...] = jnp.zeros_like(acc)
-    for stage in range(3):
-        arrive(n_steps[stage])
-        start(n_steps[stage + 1])
-    arrive(n_steps[3])
-    start(n_steps[4])
-
-    def near_body(i, _):
-        gain_block(wn, mid_lhs, (y + 3 + i // 3) % 4, (x + 3 + i % 3) % 4)
-        return 0
-
-    lax.fori_loop(0, 9, near_body, 0)
-    arrive(n_steps[4])
-
-    def far_body(i, _):
-        gain_block(wn, mid_lhs, (y + 2) % 4, i)
-        return 0
-
-    lax.fori_loop(0, 4, far_body, 0)
-
-    def side_body(i, _):
-        gain_block(wn, mid_lhs, (y + 3 + i) % 4, (x + 2) % 4)
-        return 0
-
-    lax.fori_loop(0, 3, side_body, 0)
+    for event in (1, 3, 2, 5, 4, 6, 7, 8, 9):
+        n_gather.event(event)
+    gain_all(wn, mid_lhs, n_gather)
     gain2, last_copy = gain((sy, ry), slot())
     final = mid * gain2
     fin[...] = jnp.concatenate([final, final], 0).T
@@ -561,15 +630,17 @@
     out_act[:, 128:] = jnp.where(near, fo[2], fo[3])
 
     sent([halo] + h_copies)
-    for stage in w_steps + n_steps:
-        sent(stage)
+    w_gather.all_sent()
+    n_gather.all_sent()
     for g in range(4):
         s_copy(g, s_slots[g]).wait_send()
     sent([mid_copy, last_copy] + tx_copies + ty_copies + tz_copies)
-    sent(a1 + b1 + a2 + b2 + c1 + d1 + c2 + d2 + z_copies + f_copies)
-
-
-COPIES = 120
+    for part in (ra, rb, na, nb):
+        part.all_sent()
+    sent(ring1 + ring2 + ring3 + ring4 + cy_copies + cx_copies + z_copies + f_copies)
+
+
+COPIES = 180
 
 
 def on_device(signal, templates, activations):
@@ -593,15 +664,21 @@
             f32(4, 4, 8, 64, 128),
             f32(4, 4, 8, 64, 128),
             f32(4, 4, 8, 64, 128),
-            f32(2, 2, 8, 32, 128),
-            f32(2, 2, 8, 32, 128),
-            f32(2, 4, 8, 32, 128),
-            f32(2, 4, 8, 32, 128),
-            f32(2, 4, 32, 128),
-            f32(2, 4, 32, 128),
-            f32(2, 8, 32, 128),
-            f32(2, 8, 32, 128),
-            f32(7, 64, 128),
+            f32(2, 2, 8, 24, 128),
+            f32(2, 4, 8, 24, 128),
+            f32(2, 2, 8, 24, 128),
+            f32(2, 4, 8, 24, 128),
+            f32(2, 4, 24, 128),
+            f32(2, 8, 24, 128),
+            f32(2, 4, 24, 128),
+            f32(2, 8, 24, 128),
+            f32(2, 2, 4, 16, 128),
+            f32(2, 4, 4, 16, 128),
+            f32(2, 4, 4, 16, 128),
+            f32(2, 4, 4, 16, 128),
+            f32(3, 4, 16, 128),
+            f32(3, 16, 128),
+            f32(7, 48, 128),
             f32(144, 128),
             f32(72, 128), f32(72, 128), f32(72, 128), f32(72, 128),
             f32(8, 128),

time: 150 us -> 131 us (0.87)
  Pallas kernels: 147 us -> 128 us
    pallas_call x1, Pallas kernels: 147 us -> 128 us  [on_device(): pl.pallas_call(kernel, out_shape=(jax.ShapeDtypeStruct((8, 256), F32), ja...]
where the time goes in v2:
time: 131 us
  Pallas kernels  128 us (98%)
  local copies, waits for them, and re-layouts  2.67 us (2%)
    pallas_call x1, Pallas kernels, on_device(): pl.pallas_call(kernel, out_shape=(jax.ShapeDtypeStruct((8, 256), F32), ja...  128 us
    unnamed x2, local copies, waits for them, and re-layouts  2.67 us

profile of v2, /device:TPU:1, one launch (start us, length us, event | category | flops | bytes accessed | tf_op | source)
XLA Modules:
  0.0 131.2 jit_solution(6943663814686216223)
XLA Ops:
  0.6 127.9 %shard_map.113 = (f32[8,256]{1,0:T(8,128)}, f32[64,128]{1,0:T(8,128)}) custom-call(f32[32,256,128]{2,1,0:T(8,128)} %bitcast.1, f32[64,128]{1,0:T(8,128)} %templ.1, f32[8,256]{1,0:T(8,128)} %act.1, f32[256,128]{1,0:T(8,128)} %constant.14.clone.window, f32[256,128]{1,0:T(8,128)} %constant.15.clone.tcos, f32[256,128]{1,0:T(8,128)} %constant.16.clone.tsin, ...), custom_call_target="tpu_custom_call" | custom-call | tf_op jit(solution)/shard_map/pallas_call | solution.py:650
  128.5 1.3 copy.14
  129.8 1.4 %copy.15 = f32[64,128]{1,0:T(8,128)} copy(f32[64,128]{1,0:T(8,128)} %get-tuple-element.5) | data formatting | bytes 65536

commit v3 on v2

--- a/solution.py
+++ b/solution.py
@@ -133,18 +133,24 @@
         other = (z + d) % 8
         return (other // 2 * 2 + b, other % 2 * 16 + x * 4 + y)
 
-    def at_f(d):
-        return ((f + d) % 8, t)
-
     def at_line(d):
         place = (t * 8 + f + d + 256) % 256
         return (place % 8, place // 8)
 
     greet = [partner] + [at_x(d) for d in (1, 2, 3)] + [at_y(d) for d in (1, 2, 3)]
-    greet += [at_z(d) for d in range(1, 8)] + [at_f(d) for d in range(1, 8)] + [at_line(-1), at_line(1)]
+    greet += [at_z(d) for d in range(1, 8)] + [at_line(-1), at_line(1)]
     barrier = pltpu.get_barrier_semaphore()
     for device in greet:
         pl.semaphore_signal(barrier, inc=1, device_id=device, device_id_type=MESH)
+    loads = [
+        pltpu.make_async_copy(sig_hbm.at[pl.ds(8 * i, 8)], sigv.at[pl.ds(8 * i, 8)], lsem.at[i]) for i in range(4)
+    ]
+    for load in loads:
+        load.start()
+    flip = y // 2
+    w[y, x, z] = moved(templ[...], perms[2 * flip])
+    hg[pl.ds(f, 1)] = act[...][None]
+    zrow[...] = jnp.zeros_like(zrow)
     pl.semaphore_wait(barrier, len(greet))
 
     used = [0]
@@ -159,20 +165,34 @@
             device_id=device, device_id_type=MESH,
         )
 
-    loads = [
-        pltpu.make_async_copy(sig_hbm.at[pl.ds(8 * i, 8)], sigv.at[pl.ds(8 * i, 8)], lsem.at[i]) for i in range(4)
-    ]
-    for load in loads:
-        load.start()
+    class Group:
+        def __init__(self, index, like, *copies):
+            self.index, self.like = index, like
+            self.copies = [remote(src, dst, index, device) for src, dst, device in copies]
+
+        def start(self, *which):
+            for i in which or range(len(self.copies)):
+                self.copies[i].start()
+
+        def arrive(self):
+            pltpu.make_async_copy(self.like, self.like, rsem.at[self.index]).wait()
+
+        def sent(self):
+            pltpu.make_async_copy(self.like, self.like, ssem.at[self.index]).wait()
+
+    groups = []
+
+    def group(like, *copies):
+        groups.append(Group(slot(), like, *copies))
+        return groups[-1]
+
     halo = remote(sig_hbm.at[0], sigv.at[32], slot(), at_line(-1))
     halo.start()
-    h_copies = [remote(act, hg.at[f], slot(), at_f(d)) for d in range(1, 8)]
-    for copy in h_copies:
-        copy.start()
-    hg[pl.ds(f, 1)] = act[...][None]
-
-    flip = y // 2
-    w[y, x, z] = moved(templ[...], perms[2 * flip])
+    h_far = group(hg.at[pl.ds(0, 3)], *[(act, hg.at[f], at_z(d)) for d in (2, 4, 6)])
+    h_near = group(hg.at[0], (act, hg.at[f], partner))
+    h_pass = group(hg.at[pl.ds(0, 3)], *[(hg.at[(f + d) % 8], hg.at[(f + d) % 8], partner) for d in (2, 4, 6)])
+    h_far.start()
+    h_near.start()
 
     lo, hi, low_rows = pl.ds(0, 24), pl.ds(24, 24), pl.ds(0, 48)
     end = pl.ds(48, 16)
@@ -182,87 +202,6 @@
     yl, yr, yo = (y + 3) % 4, (y + 1) % 4, (y + 2) % 4
     xl, xr, xo = (x + 3) % 4, (x + 1) % 4, (x + 2) % 4
 
-    def same(region, device):
-        return remote(region, region, slot(), device)
-
-    class Gather:
-        def __init__(self, buf):
-            self.zc = [same(buf.at[y, x, z, low_rows], at_z(d)) for d in range(1, 8)]
-            self.cx = [same(buf.at[y, x, z, end], at_x(d)) for d in (1, 2, 3)]
-            self.cy = [same(buf.at[y, every, z, end], at_y(d)) for d in (1, 2, 3)]
-            self.cz = []
-            for k in range(4):
-                right, left = (z + 8 - k) % 8, (z + k) % 8
-                parts = ((0, 1), (1, 0)) if k < 3 else ((0,), (1,))
-                ring = []
-                for i in range(len(parts[0])):
-                    ring.append(same(buf.at[half[parts[0][i]], every, right, end], at_z(1)))
-                    ring.append(same(buf.at[half[parts[1][i]], every, left, end], at_z(7)))
-                self.cz.append(ring)
-            a_own, b_own = buf.at[y, x, every, lo], buf.at[y, x, every, hi]
-            self.m1 = [same(a_own, at_x(1)), same(a_own, at_x(3)), same(b_own, at_y(1)), same(b_own, at_y(3))]
-            self.m2 = [
-                same(buf.at[y, xl, quad[0], lo], at_x(1)), same(buf.at[y, xr, quad[1], lo], at_x(3)),
-                same(buf.at[yl, x, quad[0], hi], at_y(1)), same(buf.at[yr, x, quad[1], hi], at_y(3)),
-            ]
-
-            def heavy(first_half):
-                right, left = (0, 1) if first_half else (1, 0)
-                return [
-                    same(buf.at[y, half[right], every, lo], at_y(1)), same(buf.at[y, half[left], every, lo], at_y(3)),
-                    same(buf.at[half[right], x, every, hi], at_x(1)), same(buf.at[half[left], x, every, hi], at_x(3)),
-                ]
-
-            self.h1, self.h1b = heavy(True), heavy(False)
-            self.h2 = [
-                same(buf.at[yl, half[0], every, lo], at_y(1)), same(buf.at[yr, half[1], every, lo], at_y(3)),
-                same(buf.at[half[0], xl, every, hi], at_x(1)), same(buf.at[half[1], xr, every, hi], at_x(3)),
-            ]
-
-        def event(self, k):
-            if k == 0:
-                start(self.cx)
-                start(self.zc)
-            elif k == 1:
-                arrive(self.cx)
-                start(self.cy)
-            elif k == 2:
-                arrive(self.zc)
-                start(self.m1)
-            elif k == 3:
-                arrive(self.cy)
-                start(self.cz[0])
-            elif k == 4:
-                arrive(self.m1)
-                start(self.m2)
-            elif k == 5:
-                self.ring(1)
-            elif k == 6:
-                arrive(self.m2)
-                start(self.h1)
-                start(self.h1b)
-            elif k == 7:
-                self.ring(2)
-            elif k == 8:
-                arrive(self.h1)
-                start(self.h2)
-            elif k == 9:
-                self.ring(3)
-            elif k == 10:
-                arrive(self.cz[3])
-                arrive(self.h1b)
-            else:
-                arrive(self.h2)
-
-        def ring(self, k):
-            for i in range(0, 4, 2):
-                arrive(self.cz[k - 1][i:i + 2])
-                start(self.cz[k][i:i + 2])
-
-        def all_sent(self):
-            for copies in [self.zc, self.cx, self.cy] + self.cz + [self.m1, self.m2, self.h1, self.h1b, self.h2]:
-                sent(copies)
-
     def start(copies):
         for copy in copies:
             copy.start()
@@ -275,22 +214,103 @@
         for copy in copies:
             copy.wait_send()
 
+    gather_slots = [slot() for _ in range(18)]
+
+    class Gather:
+        def __init__(self, buf):
+            count = [0]
+
+            def stage(like, *moves):
+                count[0] += 1
+                return Group(gather_slots[count[0] - 1], like, *[(region, region, device) for region, device in moves])
+
+            up, down, right, left = at_y(1), at_y(3), at_x(1), at_x(3)
+            self.zc = stage(rz, *[(buf.at[y, x, z, low_rows], at_z(d)) for d in range(1, 8)])
+            self.cx = stage(cxb, *[(buf.at[y, x, z, end], at_x(d)) for d in (1, 2, 3)])
+            self.cy = stage(cyb, *[(buf.at[y, every, z, end], at_y(d)) for d in (1, 2, 3)])
+            self.cz = []
+            for k in range(4):
+                after, before = (z + 8 - k) % 8, (z + k) % 8
+                ring = []
+                for p, q in ((0, 1), (1, 0)) if k < 3 else ((0, 1),):
+                    ring.append(stage(
+                        c1, (buf.at[half[p], every, after, end], at_z(1)), (buf.at[half[q], every, before, end], at_z(7)),
+                    ))
+                self.cz.append(ring)
+            two, four = buf.at[0, pl.ds(0, 2), every, lo], buf.at[0, every, every, lo]
+            eight = buf.at[pl.ds(0, 2), every, every, lo]
+            a_own, b_own = buf.at[y, x, every, lo], buf.at[y, x, every, hi]
+            self.m1 = stage(four, (a_own, right), (a_own, left), (b_own, up), (b_own, down))
+            self.m2 = stage(
+                two,
+                (buf.at[y, xl, quad[0], lo], right), (buf.at[y, xr, quad[1], lo], left),
+                (buf.at[yl, x, quad[0], hi], up), (buf.at[yr, x, quad[1], hi], down),
+            )
+            self.hp = stage(four, (a_own, up), (a_own, down), (b_own, right), (b_own, left))
+
+            def bulk(xx, yy):
+                a_part, b_part = buf.at[y, xx, every, lo], buf.at[yy, x, every, hi]
+                return [(a_part, up), (a_part, down), (b_part, right), (b_part, left)]
+
+            self.hs = stage(eight, *(bulk(xl, yl) + bulk(xr, yr)))
+            self.ho = stage(four, *bulk(xo, yo))
+            self.f1 = stage(two, (buf.at[yl, x, every, lo], up), (buf.at[y, xl, every, hi], right))
+            self.f2 = stage(
+                four,
+                (buf.at[yl, xl, every, lo], up), (buf.at[yr, xr, every, lo], down),
+                (buf.at[yl, xl, every, hi], right), (buf.at[yr, xr, every, hi], left),
+            )
+            self.f3 = stage(two, (buf.at[yr, xo, every, lo], down), (buf.at[yo, xr, every, hi], left))
+            self.stages = [self.zc, self.cx, self.cy] + sum(self.cz, [])
+            self.stages += [self.m1, self.m2, self.hp, self.hs, self.ho, self.f1, self.f2, self.f3]
+
+        def event(self, k):
+            after = {
+                1: (self.cx, self.cy), 2: (self.zc, self.m1, self.hp), 3: (self.cy, *self.cz[0]),
+                4: (self.m1, self.m2, self.hs), 5: (self.hp, self.f1), 7: (self.m2, self.ho),
+                9: (self.hs, self.f2), 11: (self.ho, self.f3),
+            }
+            if k in after:
+                after[k][0].arrive()
+                for stage in after[k][1:]:
+                    stage.start()
+            elif k in (6, 8, 10):
+                ring = k // 2 - 2
+                for i in range(2):
+                    self.cz[ring - 1][i].arrive()
+                    if i < len(self.cz[ring]):
+                        self.cz[ring][i].start()
+            elif k == 12:
+                self.cz[3][0].arrive()
+            else:
+                self.f1.arrive()
+                self.f2.arrive()
+                self.f3.arrive()
+
+        def all_sent(self):
+            for stage in self.stages:
+                stage.sent()
+
     w_gather = Gather(w)
-    w_gather.event(0)
+    w_gather.cx.start()
+    w_gather.zc.start()
     s_slots = [slot() for _ in range(4)]
 
     def s_copy(group, index):
         return remote(tsend.at[group], sg.at[4 * b + group], index, partner)
-
-    zrow[...] = jnp.zeros_like(zrow)
 
     def pair_step(group, p):
         n = group * 8 + 2 * p
         step = group * 4 + p
-        for when, event in ((3, 1), (6, 2), (7, 3), (10, 4), (12, 5), (14, 6)):
+        for when, event in ((3, 1), (5, 2), (6, 3), (8, 4), (10, 5), (11, 6), (12, 7), (14, 8)):
             @pl.when(step == when)
             def _(event=event):
                 w_gather.event(event)
+
+        @pl.when(step == 7)
+        def _():
+            h_far.arrive()
+            h_pass.start()
 
         win = window[...]
         h0, h1, h2 = sigv[n], sigv[n + 1], sigv[n + 2]
@@ -380,7 +400,8 @@
 
     lax.fori_loop(0, 4, group_step, 0)
 
-    arrive(h_copies)
+    h_near.arrive()
+    h_pass.arrive()
     rows64 = hg[...].reshape(64, 256)
     ht[...] = jnp.concatenate([rows64, rows64], 0).T
     h2 = ht[pl.ds(pl.multiple_of(64 * z_hi, 64), 64), :]
@@ -433,13 +454,13 @@
             gain_block(buf, lhs, (y + 3 + i) % 4, (x + 2) % 4)
             return 0
 
-        gather.event(10)
+        gather.event(12)
         lax.fori_loop(0, 9, near_body, 0)
-        gather.event(11)
+        gather.event(13)
         lax.fori_loop(0, 4, far_body, 0)
         lax.fori_loop(0, 3, side_body, 0)
 
-    for event in (7, 8, 9):
+    for event in (9, 10, 11):
         w_gather.event(event)
     gain_all(w, lhs1, w_gather)
     gain1, mid_copy = gain((sx, rx), slot())
@@ -449,8 +470,8 @@
     mid_left = doubled(mid_t[:64])
 
     tsx[...] = jnp.broadcast_to(jnp.sum(mid, axis=0, keepdims=True), (8, 128))
-    tx_copies = [remote(tsx, trx.at[d - 1], slot(), at_x(d)) for d in (1, 2, 3)]
-    start(tx_copies)
+    tx_copies = group(trx, *[(tsx, trx.at[d - 1], at_x(d)) for d in (1, 2, 3)])
+    tx_copies.start()
 
     def num_block(yy, xx):
         ratio, _, _ = ratio_of(w, mid_lhs, yy, xx)
@@ -469,81 +490,94 @@
     def run(count, blocks):
         lax.fori_loop(0, count, num_run(blocks), 0)
 
-    class Reduce4:
-        def __init__(self, get, once, twice, places, right, left):
-            own, right_place, left_place, far = places
-            self.get, self.once, self.twice, self.places = get, once, twice, places
-
-            def to(buf, side, part):
-                return buf.at[side] if part is None else buf.at[side, part]
-
-            self.first = [
-                remote(get(far, 0), once.at[0], slot(), right), remote(get(far, 1), once.at[1], slot(), left),
-            ]
-            size = once.shape[1]
-            parts = (pl.ds(0, size), pl.ds(size, size))
-            self.early = [
-                remote(get(right_place, 1), to(twice, 0, parts[1]), slot(), right),
-                remote(get(left_place, 0), to(twice, 1, parts[0]), slot(), left),
-            ]
-            self.late = [
-                remote(get(right_place, 0), to(twice, 0, parts[0]), slot(), right),
-                remote(get(left_place, 1), to(twice, 1, parts[1]), slot(), left),
-            ]
-
-        def pass_on(self):
-            own, right_place, left_place, far = self.places
-            arrive(self.first)
-            target = self.get(right_place, 0)
-            target[...] = target[...] + self.once[0]
-            target = self.get(left_place, 1)
-            target[...] = target[...] + self.once[1]
-            start(self.late)
-
-        def finish(self):
-            arrive(self.early)
-            arrive(self.late)
-            target = self.get(self.places[0], None)
-            target[...] = target[...] + (self.twice[0] + self.twice[1])
-
-        def all_sent(self):
-            sent(self.first + self.early + self.late)
-
-    def pick(parts, part):
-        return every if part is None else parts[part]
-
-    y_places, x_places = (y, yr, yl, yo), (x, xr, xl, xo)
-    ra = Reduce4(lambda i, p: num.at[i, pick(half, p), every, lo], ha1, ha2, y_places, at_y(1), at_y(3))
-    rb = Reduce4(lambda i, p: num.at[pick(half, p), i, every, hi], hb1, hb2, x_places, at_x(1), at_x(3))
-    na = Reduce4(lambda i, p: num.at[y, i, pick(quad, p), lo], ma1, ma2, x_places, at_x(1), at_x(3))
-    nb = Reduce4(lambda i, p: num.at[i, x, pick(quad, p), hi], mb1, mb2, y_places, at_y(1), at_y(3))
+    def part_a(place, part, rows=every):
+        return num.at[place, part, rows, lo]
+
+    def part_b(place, part, rows=every):
+        return num.at[part, place, rows, hi]
+
+    two, four = num.at[0, pl.ds(0, 2), every, lo], num.at[0, every, every, lo]
+    colours = (
+        (part_a, (y, yr, yl, yo), (x, xr, xl, xo), ha1, ha2, at_y(1), at_y(3)),
+        (part_b, (x, xr, xl, xo), (y, yr, yl, yo), hb1, hb2, at_x(1), at_x(3)),
+    )
+    travels = {3: 0, 2: 0, 1: 1, 0: 1}
+
+    def wave(like, moves):
+        copies = []
+        for get, places, parts, once, twice, right, left in colours:
+            for place, part, side in moves:
+                target = once.at[part] if place == 3 else twice.at[side, part]
+                copies.append((get(places[place], parts[part]), target, right if side == 0 else left))
+        return group(like, *copies)
+
+    w1 = wave(four, ((3, 3, 0), (3, 1, 1)))
+    w2 = wave(four, ((3, 2, 0), (3, 0, 1)))
+    e1 = wave(four, ((1, 1, 0), (2, 3, 1)))
+    e2 = wave(four, ((1, 0, 0), (2, 2, 1)))
+    l1 = wave(four, ((1, 3, 0), (2, 1, 1)))
+    l2 = wave(four, ((1, 2, 0), (2, 0, 1)))
+
+    def pass_on(parts_now):
+        for get, places, parts, once, twice, right, left in colours:
+            for part in parts_now:
+                target = get(places[1 + travels[part]], parts[part])
+                target[...] = target[...] + once[part]
+
+    def settle(parts_now):
+        for get, places, parts, once, twice, right, left in colours:
+            for part in parts_now:
+                target = get(places[0], parts[part])
+                target[...] = target[...] + (twice[0, part] + twice[1, part])
+
+    def mid_moves(like, moves):
+        copies = []
+        for (get, places, parts, _, _, _, _), (once, twice), right, left in (
+            (colours[0], (ma1, ma2), at_x(1), at_x(3)), (colours[1], (mb1, mb2), at_y(1), at_y(3)),
+        ):
+            for part, h, side in moves:
+                target = once.at[side] if part == 3 else twice.at[side, quad[h]]
+                copies.append((get(places[0], parts[part], quad[h]), target, right if side == 0 else left))
+        return group(like, *copies)
+
+    mf = mid_moves(two, ((3, 0, 0), (3, 1, 1)))
+    me1 = mid_moves(num.at[0, 0, every, lo], ((1, 1, 0),))
+    me2 = mid_moves(num.at[0, 0, every, lo], ((2, 0, 1),))
+    ml = mid_moves(two, ((1, 0, 0), (2, 1, 1)))
+
+    def chosen(order):
+        def blocks(i):
+            dy = sum(jnp.where(i == k, v[0], 0) for k, v in enumerate(order))
+            dx = sum(jnp.where(i == k, v[1], 0) for k, v in enumerate(order))
+            return dy, dx
+        run(len(order), blocks)
 
     run(4, lambda i: (2, i))
-    start(ra.first)
+    w1.start(0, 1)
+    w2.start(0, 1)
     run(3, lambda i: ((i + 3) % 4, 2))
-    start(rb.first)
-    run(3, lambda i: (1, (i + 3) % 4))
-    run(3, lambda i: (3, (i + 3) % 4))
-    start(ra.early)
-    run(2, lambda i: (0, 1 + 2 * i))
-    start(rb.early)
-    run(1, lambda i: (0, 0))
+    w1.start(2, 3)
+    w2.start(2, 3)
+    chosen([(1, 1), (1, 0), (3, 3), (0, 1)])
+    e1.start()
+    e2.start()
+    chosen([(1, 3), (3, 1), (3, 0), (0, 3), (0, 0)])
 
     def zz(d):
         return (z + 8 + d) % 8
 
-    ring1 = [
-        remote(num.at[half[0], every, zz(4), end], c1.at[0], slot(), at_z(1)),
-        remote(num.at[half[1], every, zz(4), end], c1.at[1], slot(), at_z(7)),
-    ]
-    start(ring1)
+    ring1 = group(
+        c1,
+        (num.at[half[0], every, zz(4), end], c1.at[0], at_z(1)), (num.at[half[1], every, zz(4), end], c1.at[1], at_z(7)),
+    )
+    ring1.start()
 
     def ring_send(buf, d):
-        copies = [
-            remote(num.at[every, every, zz(d), end], buf.at[0], slot(), at_z(1)),
-            remote(num.at[every, every, zz(-d), end], buf.at[1], slot(), at_z(7)),
-        ]
-        start(copies)
+        copies = group(
+            buf,
+            (num.at[every, every, zz(d), end], buf.at[0], at_z(1)), (num.at[every, every, zz(-d), end], buf.at[1], at_z(7)),
+        )
+        copies.start()
         return copies
 
     def ring_add(buf, d):
@@ -551,105 +585,127 @@
             target = num.at[every, every, place, end]
             target[...] = target[...] + buf[side]
 
-    arrive(tx_copies)
+    tx_copies.arrive()
     tsy[...] = tsx[...] + trx[0] + trx[1] + trx[2]
-    ty_copies = [remote(tsy, try_.at[d - 1], slot(), at_y(d)) for d in (1, 2, 3)]
-    start(ty_copies)
-    arrive(ring1)
+    ty_copies = group(try_, *[(tsy, try_.at[d - 1], at_y(d)) for d in (1, 2, 3)])
+    ty_copies.start()
+    w1.arrive()
+    pass_on((3, 1))
+    l1.start()
+    ring1.arrive()
     for side, place in ((0, zz(3)), (1, zz(-3))):
         target = num.at[half[side], every, place, end]
         target[...] = target[...] + c1[side]
     ring2 = ring_send(c2, 3)
-    ra.pass_on()
-    rb.pass_on()
-    arrive(ty_copies)
+    w2.arrive()
+    pass_on((2, 0))
+    l2.start()
+    ty_copies.arrive()
     tsz[...] = tsy[...] + try_[0] + try_[1] + try_[2]
-    tz_copies = [remote(tsz, trz.at[d - 1], slot(), at_z(d)) for d in range(1, 8)]
-    start(tz_copies)
-    arrive(ring2)
+    tz_copies = group(trz, *[(tsz, trz.at[d - 1], at_z(d)) for d in range(1, 8)])
+    tz_copies.start()
+    ring2.arrive()
     ring_add(c2, 2)
     ring3 = ring_send(c3, 2)
-    arrive(ring3)
+    e1.arrive()
+    ring3.arrive()
     ring_add(c3, 1)
     ring4 = ring_send(c4, 1)
-    ra.finish()
-    start(na.first + na.early)
-    rb.finish()
-    start(nb.first + nb.early)
-    arrive(ring4)
+    l1.arrive()
+    settle((3, 1))
+    mf.start()
+    me1.start()
+    e2.arrive()
+    l2.arrive()
+    settle((2, 0))
+    me2.start()
+    ring4.arrive()
     target = num.at[every, every, z, end]
     target[...] = target[...] + (c4[0] + c4[1])
-    cy_copies = [remote(num.at[(y + d) % 4, every, z, end], cyb.at[d - 1], slot(), at_y(d)) for d in (1, 2, 3)]
-    start(cy_copies)
-    na.pass_on()
-    nb.pass_on()
-    arrive(tz_copies)
+    cy_copies = group(cyb, *[(num.at[(y + d) % 4, every, z, end], cyb.at[d - 1], at_y(d)) for d in (1, 2, 3)])
+    cy_copies.start()
+    mf.arrive()
+    for get, places, parts, once in ((part_a, (y,), (x, xr, xl), ma1), (part_b, (x,), (y, yr, yl), mb1)):
+        for side in (0, 1):
+            target = get(places[0], parts[1 + side], quad[side])
+            target[...] = target[...] + once[side]
+    ml.start()
+    tz_copies.arrive()
     totals = tsz[...]
     for d in range(7):
         totals = totals + trz[d]
     totals = jnp.broadcast_to(totals[:1], (128, 128)).T[:64]
-    arrive(cy_copies)
+    cy_copies.arrive()
     target = num.at[y, every, z, end]
     target[...] = target[...] + (cyb[0] + cyb[1] + cyb[2])
-    cx_copies = [remote(num.at[y, (x + d) % 4, z, end], cxb.at[d - 1], slot(), at_x(d)) for d in (1, 2, 3)]
-    start(cx_copies)
-    na.finish()
-    nb.finish()
-    z_copies = [remote(num.at[y, x, zz(d), low_rows], rz.at[d - 1], slot(), at_z(d)) for d in range(1, 8)]
-    start(z_copies)
-    arrive(cx_copies)
+    cx_copies = group(cxb, *[(num.at[y, (x + d) % 4, z, end], cxb.at[d - 1], at_x(d)) for d in (1, 2, 3)])
+    cx_copies.start()
+    me1.arrive()
+    me2.arrive()
+    ml.arrive()
+    for get, place, part, twice in ((part_a, y, x, ma2), (part_b, x, y, mb2)):
+        target = get(place, part)
+        target[...] = target[...] + (twice[0] + twice[1])
+    z_copies = group(rz, *[(num.at[y, x, zz(d), low_rows], rz.at[d - 1], at_z(d)) for d in range(1, 8)])
+    z_copies.start()
+    cx_copies.arrive()
     whole = num[y, x, z, end] + (cxb[0] + cxb[1] + cxb[2])
     wn[y, x, z, end] = w[y, x, z, end] * (whole / totals[48:])
+    w_gather.all_sent()
     n_gather = Gather(wn)
-    start(n_gather.cx)
-    arrive(z_copies)
+    n_gather.cx.start()
+    z_copies.arrive()
     whole = num[y, x, z, low_rows]
     for d in range(7):
         whole = whole + rz[d]
     wn[y, x, z, low_rows] = w[y, x, z, low_rows] * (whole / totals[:48])
-    start(n_gather.zc)
+    n_gather.zc.start()
 
     out_templ[...] = moved(wn[y, x, z], perms[2 * flip + 1])
     acc[...] = jnp.zeros_like(acc)
-    for event in (1, 3, 2, 5, 4, 6, 7, 8, 9):
+    for event in (1, 3, 2, 6, 4, 5, 7, 8, 9, 10, 11):
         n_gather.event(event)
     gain_all(wn, mid_lhs, n_gather)
     gain2, last_copy = gain((sy, ry), slot())
     final = mid * gain2
     fin[...] = jnp.concatenate([final, final], 0).T
-    f_copies = []
-    for d in range(1, 4):
-        other = (z_hi + d) % 4 * 2 + b
-        rows = pl.ds(pl.multiple_of(8 * other, 8), 8)
-        f_copies.append(remote(fin.at[rows], fo.at[z_hi], slot(), (other, t)))
-    start(f_copies)
+    f_copies = group(
+        fo.at[pl.ds(0, 3)],
+        *[
+            (fin.at[pl.ds(pl.multiple_of(8 * ((f + d) % 8), 8), 8)], fo.at[z_hi], at_z(d))
+            for d in (2, 4, 6)
+        ],
+    )
+    f_copies.start()
     fo[pl.ds(z_hi, 1)] = fin[pl.ds(pl.multiple_of(8 * f, 8), 8), :][None]
-    arrive(f_copies)
-    near = lax.broadcasted_iota(jnp.int32, (8, 128), 1) < 64
-    out_act[:, :128] = jnp.where(near, fo[0], fo[1])
-    out_act[:, 128:] = jnp.where(near, fo[2], fo[3])
-
-    sent([halo] + h_copies)
-    w_gather.all_sent()
+    halo.wait_send()
     n_gather.all_sent()
     for g in range(4):
         s_copy(g, s_slots[g]).wait_send()
-    sent([mid_copy, last_copy] + tx_copies + ty_copies + tz_copies)
-    for part in (ra, rb, na, nb):
-        part.all_sent()
-    sent(ring1 + ring2 + ring3 + ring4 + cy_copies + cx_copies + z_copies + f_copies)
-
-
-COPIES = 180
+    sent([mid_copy, last_copy])
+    for part in groups:
+        part.sent()
+    f_copies.arrive()
+    out_act[...] = fo[...]
+
+
+def finish(parts, templ, out_act, out_templ):
+    near = lax.broadcasted_iota(jnp.int32, (8, 128), 1) < 64
+    out_act[:, :128] = jnp.where(near, parts[0], parts[1])
+    out_act[:, 128:] = jnp.where(near, parts[2], parts[3])
+    out_templ[...] = templ[...]
+
+
+COPIES = 64
 
 
 def on_device(signal, templates, activations):
     tables = build_tables()
     vmem = pl.BlockSpec(memory_space=pltpu.VMEM)
     f32 = lambda *shape: pltpu.VMEM(shape, F32)
-    return pl.pallas_call(
+    parts, templ = pl.pallas_call(
         kernel,
-        out_shape=(jax.ShapeDtypeStruct((8, 256), F32), jax.ShapeDtypeStruct((64, 128), F32)),
+        out_shape=(jax.ShapeDtypeStruct((4, 8, 128), F32), jax.ShapeDtypeStruct((64, 128), F32)),
         in_specs=[pl.BlockSpec(memory_space=pl.ANY)] + [vmem] * 9,
         out_specs=(vmem, vmem),
         scratch_shapes=[
@@ -664,9 +720,9 @@
             f32(4, 4, 8, 64, 128),
             f32(4, 4, 8, 64, 128),
             f32(4, 4, 8, 64, 128),
-            f32(2, 2, 8, 24, 128),
+            f32(4, 8, 24, 128),
             f32(2, 4, 8, 24, 128),
-            f32(2, 2, 8, 24, 128),
+            f32(4, 8, 24, 128),
             f32(2, 4, 8, 24, 128),
             f32(2, 4, 24, 128),
             f32(2, 8, 24, 128),
@@ -694,6 +750,12 @@
             collective_id=0, has_side_effects=True, vmem_limit_bytes=60 * 1024 * 1024
         ),
     )(signal.reshape(32, 256, 128), templates, activations, *tables)
+    return pl.pallas_call(
+        finish,
+        out_shape=(jax.ShapeDtypeStruct((8, 256), F32), jax.ShapeDtypeStruct((64, 128), F32)),
+        in_specs=[vmem, vmem],
+        out_specs=(vmem, vmem),
+    )(parts, templ)
 
 
 def solution(mesh):

time: 131 us -> 126 us (0.962)
  Pallas kernels: 128 us -> 125 us
  local copies, waits for them, and re-layouts: 2.67 us -> 0 us
    unnamed x2 -> x0, local copies, waits for them, and re-layouts: 2.67 us -> none
    pallas_call x1 -> x2, Pallas kernels: 128 us -> 125 us  [the longest x1 124 us: on_device(): pl.pallas_call(kernel, out_shape=(jax.ShapeDtypeStruct((4, 8, 128), F32),...]
where the time goes in v3:
time: 126 us
  Pallas kernels  125 us (99%)
    pallas_call x1, Pallas kernels, on_device(): pl.pallas_call(kernel, out_shape=(jax.ShapeDtypeStruct((4, 8, 128), F32),...  124 us

profile of v3, /device:TPU:1, one launch (start us, length us, event | category | flops | bytes accessed | tf_op | source)
XLA Modules:
  0.0 126.0 jit_solution(7415169210205572353)
XLA Ops:
  0.6 124.0 %shard_map.113 = (f32[4,8,128]{2,1,0:T(8,128)}, f32[64,128]{1,0:T(8,128)}) custom-call(f32[32,256,128]{2,1,0:T(8,128)} %bitcast.1, f32[64,128]{1,0:T(8,128)} %templ.1, f32[8,256]{1,0:T(8,128)} %act.1, f32[256,128]{1,0:T(8,128)} %constant.14.clone.window, f32[256,128]{1,0:T(8,128)} %constant.15.clone.tcos, f32[256,128]{1,0:T(8,128)} %constant.16.clone.tsin, ...), custom_call_target="tpu_custom_call" | custom-call | tf_op jit(solution)/shard_map/pallas_call | solution.py:706
  124.6 1.4 %shard_map.114 = (f32[8,256]{1,0:T(8,128)}, f32[64,128]{1,0:T(8,128)}) custom-call(f32[4,8,128]{2,1,0:T(8,128)} %get-tuple-element.4.parts, f32[64,128]{1,0:T(8,128)} %get-tuple-element.5.templ), custom_call_target="tpu_custom_call" | custom-call | tf_op jit(solution)/shard_map/pallas_call | solution.py:753

commit v4 on v3

--- a/solution.py
+++ b/solution.py
@@ -110,7 +110,7 @@
     out_act, out_templ,
     sigv, hg, ht, mag, zrow, mag0, sg, tsend, w, wn, num,
     ha1, ha2, hb1, hb2, ma1, ma2, mb1, mb2, c1, c2, c3, c4, cyb, cxb, rz,
-    acc, sx, rx, sy, ry, tsx, trx, try_, trz, tsy, tsz, fin, fo,
+    hop, acc, sx, rx, sy, ry, tsx, trx, try_, trz, tsy, tsz, fin, fo,
     lsem, ssem, rsem,
 ):
     f = lax.axis_index("freq")
@@ -133,12 +133,8 @@
         other = (z + d) % 8
         return (other // 2 * 2 + b, other % 2 * 16 + x * 4 + y)
 
-    def at_line(d):
-        place = (t * 8 + f + d + 256) % 256
-        return (place % 8, place // 8)
-
     greet = [partner] + [at_x(d) for d in (1, 2, 3)] + [at_y(d) for d in (1, 2, 3)]
-    greet += [at_z(d) for d in range(1, 8)] + [at_line(-1), at_line(1)]
+    greet += [at_z(d) for d in range(1, 8)]
     barrier = pltpu.get_barrier_semaphore()
     for device in greet:
         pl.semaphore_signal(barrier, inc=1, device_id=device, device_id_type=MESH)
@@ -186,15 +182,23 @@
         groups.append(Group(slot(), like, *copies))
         return groups[-1]
 
-    halo = remote(sig_hbm.at[0], sigv.at[32], slot(), at_line(-1))
-    halo.start()
+    halos = [
+        group(hop.at[0], (sig_hbm.at[0], hop.at[0], partner)),
+        group(hop.at[5], (sig_hbm.at[0], hop.at[5], at_z(6))),
+        group(hop.at[1], (hop.at[5], hop.at[1], partner)),
+        group(hop.at[2], (hop.at[1], hop.at[2], at_y(3))),
+        group(hop.at[3], (hop.at[2], hop.at[3], at_x(3))),
+        group(hop.at[4], (hop.at[3], hop.at[4], at_z(7))),
+    ]
+    halos[0].start()
+    halos[1].start()
     h_far = group(hg.at[pl.ds(0, 3)], *[(act, hg.at[f], at_z(d)) for d in (2, 4, 6)])
     h_near = group(hg.at[0], (act, hg.at[f], partner))
     h_pass = group(hg.at[pl.ds(0, 3)], *[(hg.at[(f + d) % 8], hg.at[(f + d) % 8], partner) for d in (2, 4, 6)])
     h_far.start()
     h_near.start()
 
-    lo, hi, low_rows = pl.ds(0, 24), pl.ds(24, 24), pl.ds(0, 48)
+    subs = ((0, 8), (16, 16))
     end = pl.ds(48, 16)
     half = (pl.ds(0, 2), pl.ds(2, 2))
     quad = (pl.ds(0, 4), pl.ds(4, 4))
@@ -214,86 +218,111 @@
         for copy in copies:
             copy.wait_send()
 
-    gather_slots = [slot() for _ in range(18)]
-
-    class Gather:
-        def __init__(self, buf):
-            count = [0]
-
-            def stage(like, *moves):
-                count[0] += 1
-                return Group(gather_slots[count[0] - 1], like, *[(region, region, device) for region, device in moves])
-
-            up, down, right, left = at_y(1), at_y(3), at_x(1), at_x(3)
-            self.zc = stage(rz, *[(buf.at[y, x, z, low_rows], at_z(d)) for d in range(1, 8)])
-            self.cx = stage(cxb, *[(buf.at[y, x, z, end], at_x(d)) for d in (1, 2, 3)])
-            self.cy = stage(cyb, *[(buf.at[y, every, z, end], at_y(d)) for d in (1, 2, 3)])
+    gather_slots = [slot() for _ in range(27)]
+    up, down, right, left = at_y(1), at_y(3), at_x(1), at_x(3)
+
+    class Stages:
+        def __init__(self, slots):
+            self.slots, self.stages = list(slots), []
+
+        def stage(self, like, *moves):
+            self.stages.append(Group(self.slots.pop(0), like, *[(region, region, device) for region, device in moves]))
+            return self.stages[-1]
+
+        def all_sent(self):
+            for stage in self.stages:
+                stage.sent()
+
+    class Ring(Stages):
+        def __init__(self, buf, slots):
+            super().__init__(slots)
+            self.cx = self.stage(cxb, *[(buf.at[y, x, z, end], at_x(d)) for d in (1, 2, 3)])
+            self.cy = self.stage(cyb, *[(buf.at[y, every, z, end], at_y(d)) for d in (1, 2, 3)])
             self.cz = []
             for k in range(4):
                 after, before = (z + 8 - k) % 8, (z + k) % 8
-                ring = []
-                for p, q in ((0, 1), (1, 0)) if k < 3 else ((0, 1),):
-                    ring.append(stage(
+                self.cz.append([
+                    self.stage(
                         c1, (buf.at[half[p], every, after, end], at_z(1)), (buf.at[half[q], every, before, end], at_z(7)),
-                    ))
-                self.cz.append(ring)
+                    )
+                    for p, q in (((0, 1), (1, 0)) if k < 3 else ((0, 1),))
+                ])
+
+        def event(self, k):
+            if k == 0:
+                self.cx.start()
+            elif k == 1:
+                self.cx.arrive()
+                self.cy.start()
+            elif k == 2:
+                self.cy.arrive()
+                self.cz[0][0].start()
+                self.cz[0][1].start()
+            elif k < 6:
+                for i in range(2):
+                    self.cz[k - 3][i].arrive()
+                    if i < len(self.cz[k - 2]):
+                        self.cz[k - 2][i].start()
+            else:
+                self.cz[3][0].arrive()
+
+    class Bulk(Stages):
+        def __init__(self, buf, sub, slots):
+            super().__init__(slots)
+            row, rows = sub
+            lo, hi, both = pl.ds(row, rows), pl.ds(row + rows, rows), pl.ds(row, 2 * rows)
             two, four = buf.at[0, pl.ds(0, 2), every, lo], buf.at[0, every, every, lo]
             eight = buf.at[pl.ds(0, 2), every, every, lo]
+
+            def bulk(xx, yy):
+                a_part, b_part = buf.at[y, xx, every, lo], buf.at[yy, x, every, hi]
+                return [(a_part, up), (a_part, down), (b_part, right), (b_part, left)]
+
             a_own, b_own = buf.at[y, x, every, lo], buf.at[y, x, every, hi]
-            self.m1 = stage(four, (a_own, right), (a_own, left), (b_own, up), (b_own, down))
-            self.m2 = stage(
+            zc = self.stage(rz.at[every, both], *[(buf.at[y, x, z, both], at_z(d)) for d in range(1, 8)])
+            m1 = self.stage(four, (a_own, right), (a_own, left), (b_own, up), (b_own, down))
+            hp = self.stage(four, *bulk(x, y))
+            m2 = self.stage(
                 two,
                 (buf.at[y, xl, quad[0], lo], right), (buf.at[y, xr, quad[1], lo], left),
                 (buf.at[yl, x, quad[0], hi], up), (buf.at[yr, x, quad[1], hi], down),
             )
-            self.hp = stage(four, (a_own, up), (a_own, down), (b_own, right), (b_own, left))
-
-            def bulk(xx, yy):
-                a_part, b_part = buf.at[y, xx, every, lo], buf.at[yy, x, every, hi]
-                return [(a_part, up), (a_part, down), (b_part, right), (b_part, left)]
-
-            self.hs = stage(eight, *(bulk(xl, yl) + bulk(xr, yr)))
-            self.ho = stage(four, *bulk(xo, yo))
-            self.f1 = stage(two, (buf.at[yl, x, every, lo], up), (buf.at[y, xl, every, hi], right))
-            self.f2 = stage(
+            hs = self.stage(eight, *(bulk(xl, yl) + bulk(xr, yr)))
+            ho = self.stage(four, *bulk(xo, yo))
+            f1 = self.stage(two, (buf.at[yl, x, every, lo], up), (buf.at[y, xl, every, hi], right))
+            f2 = self.stage(
                 four,
                 (buf.at[yl, xl, every, lo], up), (buf.at[yr, xr, every, lo], down),
                 (buf.at[yl, xl, every, hi], right), (buf.at[yr, xr, every, hi], left),
             )
-            self.f3 = stage(two, (buf.at[yr, xo, every, lo], down), (buf.at[yo, xr, every, hi], left))
-            self.stages = [self.zc, self.cx, self.cy] + sum(self.cz, [])
-            self.stages += [self.m1, self.m2, self.hp, self.hs, self.ho, self.f1, self.f2, self.f3]
+            f3 = self.stage(two, (buf.at[yr, xo, every, lo], down), (buf.at[yo, xr, every, hi], left))
+            self.steps = [
+                ((), (zc,)), ((zc,), (m1, hp)), ((m1,), (m2, hs)), ((hp,), (f1,)), ((m2,), (ho,)), ((hs,), (f2,)),
+                ((ho,), (f3,)), ((f1, f2, f3), ()),
+            ]
 
         def event(self, k):
-            after = {
-                1: (self.cx, self.cy), 2: (self.zc, self.m1, self.hp), 3: (self.cy, *self.cz[0]),
-                4: (self.m1, self.m2, self.hs), 5: (self.hp, self.f1), 7: (self.m2, self.ho),
-                9: (self.hs, self.f2), 11: (self.ho, self.f3),
-            }
-            if k in after:
-                after[k][0].arrive()
-                for stage in after[k][1:]:
-                    stage.start()
-            elif k in (6, 8, 10):
-                ring = k // 2 - 2
-                for i in range(2):
-                    self.cz[ring - 1][i].arrive()
-                    if i < len(self.cz[ring]):
-                        self.cz[ring][i].start()
-            elif k == 12:
-                self.cz[3][0].arrive()
-            else:
-                self.f1.arrive()
-                self.f2.arrive()
-                self.f3.arrive()
+            for stage in self.steps[k][0]:
+                stage.arrive()
+            for stage in self.steps[k][1]:
+                stage.start()
+
+    class Gather:
+        def __init__(self, buf):
+            self.parts = [
+                Ring(buf, gather_slots[:9]), Bulk(buf, subs[0], gather_slots[9:18]), Bulk(buf, subs[1], gather_slots[18:]),
+            ]
+
+        def event(self, part, k):
+            self.parts[part].event(k)
 
         def all_sent(self):
-            for stage in self.stages:
-                stage.sent()
+            for part in self.parts:
+                part.all_sent()
 
     w_gather = Gather(w)
-    w_gather.cx.start()
-    w_gather.zc.start()
+    for part in range(3):
+        w_gather.event(part, 0)
     s_slots = [slot() for _ in range(4)]
 
     def s_copy(group, index):
@@ -302,15 +331,25 @@
     def pair_step(group, p):
         n = group * 8 + 2 * p
         step = group * 4 + p
-        for when, event in ((3, 1), (5, 2), (6, 3), (8, 4), (10, 5), (11, 6), (12, 7), (14, 8)):
+        for when, events in (
+            (2, ((0, 1),)), (3, ((1, 1),)), (5, ((0, 2), (1, 2))), (6, ((1, 3),)), (7, ((2, 1), (1, 4))),
+            (9, ((0, 3), (2, 2))), (10, ((1, 5), (2, 3))), (12, ((1, 6), (2, 4))), (14, ((0, 4), (2, 5))),
+        ):
             @pl.when(step == when)
-            def _(event=event):
-                w_gather.event(event)
-
-        @pl.when(step == 7)
+            def _(events=events):
+                for event in events:
+                    w_gather.event(*event)
+
+        @pl.when(step == 4)
         def _():
             h_far.arrive()
             h_pass.start()
+
+        for when, stage in ((2, 1), (4, 2), (7, 3), (9, 4)):
+            @pl.when(step == when)
+            def _(stage=stage):
+                halos[stage].arrive()
+                halos[stage + 1].start()
 
         win = window[...]
         h0, h1, h2 = sigv[n], sigv[n + 1], sigv[n + 2]
@@ -374,8 +413,11 @@
 
         @pl.when(group == 3)
         def _():
-            halo.wait_recv()
-            sigv[32] = sigv[32] * jnp.where(t * 8 + f == 255, 0.0, 1.0)
+            halos[0].arrive()
+            halos[5].arrive()
+            line = jnp.where(y < 3, 2, jnp.where(x < 3, 3, 4))
+            source = jnp.where(b == 0, 0, jnp.where(z_hi < 3, 1, line))
+            sigv[32] = hop[source] * jnp.where(t * 8 + f == 255, 0.0, 1.0)
 
         def body(p, _):
             pair_step(group, p)
@@ -454,14 +496,15 @@
             gain_block(buf, lhs, (y + 3 + i) % 4, (x + 2) % 4)
             return 0
 
-        gather.event(12)
+        gather.event(0, 6)
         lax.fori_loop(0, 9, near_body, 0)
-        gather.event(13)
+        gather.event(1, 7)
+        gather.event(2, 7)
         lax.fori_loop(0, 4, far_body, 0)
         lax.fori_loop(0, 3, side_body, 0)
 
-    for event in (9, 10, 11):
-        w_gather.event(event)
+    w_gather.event(0, 5)
+    w_gather.event(2, 6)
     gain_all(w, lhs1, w_gather)
     gain1, mid_copy = gain((sx, rx), slot())
     mid = h2 * gain1
@@ -490,60 +533,117 @@
     def run(count, blocks):
         lax.fori_loop(0, count, num_run(blocks), 0)
 
-    def part_a(place, part, rows=every):
-        return num.at[place, part, rows, lo]
-
-    def part_b(place, part, rows=every):
-        return num.at[part, place, rows, hi]
-
-    two, four = num.at[0, pl.ds(0, 2), every, lo], num.at[0, every, every, lo]
-    colours = (
-        (part_a, (y, yr, yl, yo), (x, xr, xl, xo), ha1, ha2, at_y(1), at_y(3)),
-        (part_b, (x, xr, xl, xo), (y, yr, yl, yo), hb1, hb2, at_x(1), at_x(3)),
-    )
     travels = {3: 0, 2: 0, 1: 1, 0: 1}
 
-    def wave(like, moves):
-        copies = []
-        for get, places, parts, once, twice, right, left in colours:
-            for place, part, side in moves:
-                target = once.at[part] if place == 3 else twice.at[side, part]
-                copies.append((get(places[place], parts[part]), target, right if side == 0 else left))
-        return group(like, *copies)
-
-    w1 = wave(four, ((3, 3, 0), (3, 1, 1)))
-    w2 = wave(four, ((3, 2, 0), (3, 0, 1)))
-    e1 = wave(four, ((1, 1, 0), (2, 3, 1)))
-    e2 = wave(four, ((1, 0, 0), (2, 2, 1)))
-    l1 = wave(four, ((1, 3, 0), (2, 1, 1)))
-    l2 = wave(four, ((1, 2, 0), (2, 0, 1)))
-
-    def pass_on(parts_now):
-        for get, places, parts, once, twice, right, left in colours:
-            for part in parts_now:
-                target = get(places[1 + travels[part]], parts[part])
-                target[...] = target[...] + once[part]
-
-    def settle(parts_now):
-        for get, places, parts, once, twice, right, left in colours:
-            for part in parts_now:
-                target = get(places[0], parts[part])
-                target[...] = target[...] + (twice[0, part] + twice[1, part])
-
-    def mid_moves(like, moves):
-        copies = []
-        for (get, places, parts, _, _, _, _), (once, twice), right, left in (
-            (colours[0], (ma1, ma2), at_x(1), at_x(3)), (colours[1], (mb1, mb2), at_y(1), at_y(3)),
-        ):
-            for part, h, side in moves:
-                target = once.at[side] if part == 3 else twice.at[side, quad[h]]
-                copies.append((get(places[0], parts[part], quad[h]), target, right if side == 0 else left))
-        return group(like, *copies)
-
-    mf = mid_moves(two, ((3, 0, 0), (3, 1, 1)))
-    me1 = mid_moves(num.at[0, 0, every, lo], ((1, 1, 0),))
-    me2 = mid_moves(num.at[0, 0, every, lo], ((2, 0, 1),))
-    ml = mid_moves(two, ((1, 0, 0), (2, 1, 1)))
+    class Reduce:
+        def __init__(self, sub):
+            row, rows = sub
+            lo, hi = pl.ds(row, rows), pl.ds(row + rows, rows)
+            self.both = pl.ds(row, 2 * rows)
+            here = pl.ds(row // 2, rows)
+            one, two, four = num.at[0, 0, every, lo], num.at[0, pl.ds(0, 2), every, lo], num.at[0, every, every, lo]
+
+            def part_a(place, part, z_rows=every):
+                return num.at[place, part, z_rows, lo]
+
+            def part_b(place, part, z_rows=every):
+                return num.at[part, place, z_rows, hi]
+
+            self.colours = (
+                (part_a, (y, yr, yl, yo), (x, xr, xl, xo), ha1, ha2, ma1, ma2, up, down, right, left),
+                (part_b, (x, xr, xl, xo), (y, yr, yl, yo), hb1, hb2, mb1, mb2, right, left, up, down),
+            )
+            self.here = here
+
+            def wave(*moves):
+                copies = []
+                for get, places, parts, once, twice, _, _, ahead, behind, _, _ in self.colours:
+                    for place, part, side in moves:
+                        target = once.at[part, every, here] if place == 3 else twice.at[side, part, every, here]
+                        copies.append((get(places[place], parts[part]), target, ahead if side == 0 else behind))
+                return group(four, *copies)
+
+            self.w1, self.w2 = wave((3, 3, 0), (3, 1, 1)), wave((3, 2, 0), (3, 0, 1))
+            self.e1, self.e2 = wave((1, 1, 0), (2, 3, 1)), wave((1, 0, 0), (2, 2, 1))
+            self.l1, self.l2 = wave((1, 3, 0), (2, 1, 1)), wave((1, 2, 0), (2, 0, 1))
+
+            def mid_moves(like, *moves):
+                copies = []
+                for get, places, parts, _, _, once, twice, _, _, ahead, behind in self.colours:
+                    for part, h, side in moves:
+                        target = once.at[side, every, here] if part == 3 else twice.at[side, quad[h], here]
+                        copies.append((get(places[0], parts[part], quad[h]), target, ahead if side == 0 else behind))
+                return group(like, *copies)
+
+            self.mf = mid_moves(two, (3, 0, 0), (3, 1, 1))
+            self.me1, self.me2 = mid_moves(one, (1, 1, 0)), mid_moves(one, (2, 0, 1))
+            self.ml = mid_moves(two, (1, 0, 0), (2, 1, 1))
+            self.zs = group(
+                rz.at[every, self.both],
+                *[(num.at[y, x, zz(d), self.both], rz.at[d - 1, self.both], at_z(d)) for d in range(1, 8)],
+            )
+
+        def pass_on(self, parts_now):
+            for get, places, parts, once, *_ in self.colours:
+                for part in parts_now:
+                    target = get(places[1 + travels[part]], parts[part])
+                    target[...] = target[...] + once[part, :, self.here]
+
+        def settle(self, parts_now):
+            for get, places, parts, _, twice, *_ in self.colours:
+                for part in parts_now:
+                    target = get(places[0], parts[part])
+                    target[...] = target[...] + (twice[0, part, :, self.here] + twice[1, part, :, self.here])
+
+        def event(self, k):
+            if k == 1:
+                self.w1.arrive()
+                self.pass_on((3, 1))
+                self.l1.start()
+            elif k == 2:
+                self.w2.arrive()
+                self.pass_on((2, 0))
+                self.l2.start()
+            elif k == 3:
+                self.e1.arrive()
+                self.l1.arrive()
+                self.settle((3, 1))
+                self.mf.start()
+                self.me1.start()
+            elif k == 4:
+                self.e2.arrive()
+                self.l2.arrive()
+                self.settle((2, 0))
+                self.me2.start()
+            elif k == 5:
+                self.mf.arrive()
+                for get, places, parts, _, _, once, *_ in self.colours:
+                    for side in (0, 1):
+                        target = get(places[0], parts[1 + side], quad[side])
+                        target[...] = target[...] + once[side, :, self.here]
+                self.ml.start()
+            elif k == 6:
+                self.me1.arrive()
+                self.me2.arrive()
+                self.ml.arrive()
+                for get, places, parts, _, _, _, twice, *_ in self.colours:
+                    target = get(places[0], parts[0])
+                    target[...] = target[...] + (twice[0, :, self.here] + twice[1, :, self.here])
+                self.zs.start()
+            else:
+                self.zs.arrive()
+                whole = num[y, x, z, self.both]
+                for d in range(7):
+                    whole = whole + rz[d, self.both]
+                row, rows = self.both.start, self.both.size
+                wn[y, x, z, self.both] = w[y, x, z, self.both] * (whole / totals[row:row + rows])
+
+    def zz(d):
+        return (z + 8 + d) % 8
+
+    w_gather.all_sent()
+    n_gather = Gather(wn)
+    r1, r2 = Reduce(subs[0]), Reduce(subs[1])
 
     def chosen(order):
         def blocks(i):
@@ -553,18 +653,16 @@
         run(len(order), blocks)
 
     run(4, lambda i: (2, i))
-    w1.start(0, 1)
-    w2.start(0, 1)
+    r1.w1.start(0, 1)
+    r1.w2.start(0, 1)
     run(3, lambda i: ((i + 3) % 4, 2))
-    w1.start(2, 3)
-    w2.start(2, 3)
+    r1.w1.start(2, 3)
+    r1.w2.start(2, 3)
     chosen([(1, 1), (1, 0), (3, 3), (0, 1)])
-    e1.start()
-    e2.start()
+    r1.e1.start()
+    r1.e2.start()
+    r2.w1.start()
     chosen([(1, 3), (3, 1), (3, 0), (0, 3), (0, 0)])
-
-    def zz(d):
-        return (z + 8 + d) % 8
 
     ring1 = group(
         c1,
@@ -589,82 +687,70 @@
     tsy[...] = tsx[...] + trx[0] + trx[1] + trx[2]
     ty_copies = group(try_, *[(tsy, try_.at[d - 1], at_y(d)) for d in (1, 2, 3)])
     ty_copies.start()
-    w1.arrive()
-    pass_on((3, 1))
-    l1.start()
+    r1.event(1)
+    r2.w2.start()
     ring1.arrive()
     for side, place in ((0, zz(3)), (1, zz(-3))):
         target = num.at[half[side], every, place, end]
         target[...] = target[...] + c1[side]
     ring2 = ring_send(c2, 3)
-    w2.arrive()
-    pass_on((2, 0))
-    l2.start()
+    r1.event(2)
+    r2.e1.start()
     ty_copies.arrive()
     tsz[...] = tsy[...] + try_[0] + try_[1] + try_[2]
     tz_copies = group(trz, *[(tsz, trz.at[d - 1], at_z(d)) for d in range(1, 8)])
     tz_copies.start()
+    r1.event(3)
+    r2.event(1)
+    r2.e2.start()
     ring2.arrive()
     ring_add(c2, 2)
     ring3 = ring_send(c3, 2)
-    e1.arrive()
+    r1.event(4)
+    r2.event(2)
+    r1.event(5)
+    tz_copies.arrive()
+    totals = tsz[...]
+    for d in range(7):
+        totals = totals + trz[d]
+    totals = jnp.broadcast_to(totals[:1], (128, 128)).T[:64]
     ring3.arrive()
     ring_add(c3, 1)
     ring4 = ring_send(c4, 1)
-    l1.arrive()
-    settle((3, 1))
-    mf.start()
-    me1.start()
-    e2.arrive()
-    l2.arrive()
-    settle((2, 0))
-    me2.start()
+    r1.event(6)
+    r2.event(3)
     ring4.arrive()
     target = num.at[every, every, z, end]
     target[...] = target[...] + (c4[0] + c4[1])
     cy_copies = group(cyb, *[(num.at[(y + d) % 4, every, z, end], cyb.at[d - 1], at_y(d)) for d in (1, 2, 3)])
     cy_copies.start()
-    mf.arrive()
-    for get, places, parts, once in ((part_a, (y,), (x, xr, xl), ma1), (part_b, (x,), (y, yr, yl), mb1)):
-        for side in (0, 1):
-            target = get(places[0], parts[1 + side], quad[side])
-            target[...] = target[...] + once[side]
-    ml.start()
-    tz_copies.arrive()
-    totals = tsz[...]
-    for d in range(7):
-        totals = totals + trz[d]
-    totals = jnp.broadcast_to(totals[:1], (128, 128)).T[:64]
+    r1.event(7)
+    n_gather.event(1, 0)
+    r2.event(4)
     cy_copies.arrive()
     target = num.at[y, every, z, end]
     target[...] = target[...] + (cyb[0] + cyb[1] + cyb[2])
     cx_copies = group(cxb, *[(num.at[y, (x + d) % 4, z, end], cxb.at[d - 1], at_x(d)) for d in (1, 2, 3)])
     cx_copies.start()
-    me1.arrive()
-    me2.arrive()
-    ml.arrive()
-    for get, place, part, twice in ((part_a, y, x, ma2), (part_b, x, y, mb2)):
-        target = get(place, part)
-        target[...] = target[...] + (twice[0] + twice[1])
-    z_copies = group(rz, *[(num.at[y, x, zz(d), low_rows], rz.at[d - 1], at_z(d)) for d in range(1, 8)])
-    z_copies.start()
+    r2.event(5)
+    n_gather.event(1, 1)
     cx_copies.arrive()
     whole = num[y, x, z, end] + (cxb[0] + cxb[1] + cxb[2])
     wn[y, x, z, end] = w[y, x, z, end] * (whole / totals[48:])
-    w_gather.all_sent()
-    n_gather = Gather(wn)
-    n_gather.cx.start()
-    z_copies.arrive()
-    whole = num[y, x, z, low_rows]
-    for d in range(7):
-        whole = whole + rz[d]
-    wn[y, x, z, low_rows] = w[y, x, z, low_rows] * (whole / totals[:48])
-    n_gather.zc.start()
+    n_gather.event(0, 0)
+    r2.event(6)
+    n_gather.event(1, 2)
+    n_gather.event(1, 3)
+    n_gather.event(0, 1)
+    r2.event(7)
+    n_gather.event(2, 0)
 
     out_templ[...] = moved(wn[y, x, z], perms[2 * flip + 1])
     acc[...] = jnp.zeros_like(acc)
-    for event in (1, 3, 2, 6, 4, 5, 7, 8, 9, 10, 11):
-        n_gather.event(event)
+    for event in (
+        (1, 4), (0, 2), (1, 5), (1, 6), (2, 1), (0, 3), (2, 2), (2, 3), (0, 4), (2, 4), (2, 5), (0, 5), (2, 6),
+    ):
+        n_gather.event(*event)
     gain_all(wn, mid_lhs, n_gather)
     gain2, last_copy = gain((sy, ry), slot())
     final = mid * gain2
@@ -678,7 +764,6 @@
     )
     f_copies.start()
     fo[pl.ds(z_hi, 1)] = fin[pl.ds(pl.multiple_of(8 * f, 8), 8), :][None]
-    halo.wait_send()
     n_gather.all_sent()
     for g in range(4):
         s_copy(g, s_slots[g]).wait_send()
@@ -696,7 +781,7 @@
     out_templ[...] = templ[...]
 
 
-COPIES = 64
+COPIES = 96
 
 
 def on_device(signal, templates, activations):
@@ -735,6 +820,7 @@
             f32(3, 4, 16, 128),
             f32(3, 16, 128),
             f32(7, 48, 128),
+            f32(6, 256, 128),
             f32(144, 128),
             f32(72, 128), f32(72, 128), f32(72, 128), f32(72, 128),
             f32(8, 128),

time: 126 us -> 136 us (1.079)
  Pallas kernels: 125 us -> 135 us
    pallas_call x1, Pallas kernels: 124 us -> 134 us  [on_device(): pl.pallas_call(kernel, out_shape=(jax.ShapeDtypeStruct((4, 8, 128), F32),...]
where the time goes in v4:
time: 136 us
  Pallas kernels  135 us (99%)
    pallas_call x1, Pallas kernels, on_device(): pl.pallas_call(kernel, out_shape=(jax.ShapeDtypeStruct((4, 8, 128), F32),...  134 us

profile of v4, /device:TPU:1, one launch (start us, length us, event | category | flops | bytes accessed | tf_op | source)
XLA Modules:
  0.0 135.6 jit_solution(15290732366302598105)
XLA Ops:
  0.6 133.6 %shard_map.113 = (f32[4,8,128]{2,1,0:T(8,128)}, f32[64,128]{1,0:T(8,128)}) custom-call(f32[32,256,128]{2,1,0:T(8,128)} %bitcast.1, f32[64,128]{1,0:T(8,128)} %templ.1, f32[8,256]{1,0:T(8,128)} %act.1, f32[256,128]{1,0:T(8,128)} %constant.14.clone.window, f32[256,128]{1,0:T(8,128)} %constant.15.clone.tcos, f32[256,128]{1,0:T(8,128)} %constant.16.clone.tsin, ...), custom_call_target="tpu_custom_call" | custom-call | tf_op jit(solution)/shard_map/pallas_call | solution.py:791
  134.2 1.4 %shard_map.114 = (f32[8,256]{1,0:T(8,128)}, f32[64,128]{1,0:T(8,128)}) custom-call(f32[4,8,128]{2,1,0:T(8,128)} %get-tuple-element.4.parts, f32[64,128]{1,0:T(8,128)} %get-tuple-element.5.templ), custom_call_target="tpu_custom_call" | custom-call | tf_op jit(solution)/shard_map/pallas_call | solution.py:839

commit v5 on v3

--- a/solution.py
+++ b/solution.py
@@ -110,7 +110,7 @@
     out_act, out_templ,
     sigv, hg, ht, mag, zrow, mag0, sg, tsend, w, wn, num,
     ha1, ha2, hb1, hb2, ma1, ma2, mb1, mb2, c1, c2, c3, c4, cyb, cxb, rz,
-    acc, sx, rx, sy, ry, tsx, trx, try_, trz, tsy, tsz, fin, fo,
+    hop, acc, sx, rx, sy, ry, tsx, trx, try_, trz, tsy, tsz, fin, fo,
     lsem, ssem, rsem,
 ):
     f = lax.axis_index("freq")
@@ -133,12 +133,8 @@
         other = (z + d) % 8
         return (other // 2 * 2 + b, other % 2 * 16 + x * 4 + y)
 
-    def at_line(d):
-        place = (t * 8 + f + d + 256) % 256
-        return (place % 8, place // 8)
-
     greet = [partner] + [at_x(d) for d in (1, 2, 3)] + [at_y(d) for d in (1, 2, 3)]
-    greet += [at_z(d) for d in range(1, 8)] + [at_line(-1), at_line(1)]
+    greet += [at_z(d) for d in range(1, 8)]
     barrier = pltpu.get_barrier_semaphore()
     for device in greet:
         pl.semaphore_signal(barrier, inc=1, device_id=device, device_id_type=MESH)
@@ -186,8 +182,31 @@
         groups.append(Group(slot(), like, *copies))
         return groups[-1]
 
-    halo = remote(sig_hbm.at[0], sigv.at[32], slot(), at_line(-1))
-    halo.start()
+    turn_y = (b == 1) & (z_hi == 3)
+    turn_x = turn_y & (y == 3)
+    turn_z = turn_x & (x == 3)
+    halos = [
+        (sig_hbm.at[0], hop.at[0], partner, b == 1, b == 0),
+        (sig_hbm.at[0], hop.at[5], at_z(6), b == 0, b == 0),
+        (hop.at[5], hop.at[1], partner, b == 0, b == 1),
+        (hop.at[1], hop.at[2], at_y(3), turn_y, turn_y),
+        (hop.at[2], hop.at[3], at_x(3), turn_x, turn_x),
+        (hop.at[3], hop.at[4], at_z(7), turn_z & (z_lo == 1), turn_z & (z_lo == 0)),
+    ]
+    halos = [(remote(src, dst, slot(), device), sends, receives) for src, dst, device, sends, receives in halos]
+
+    def halo_start(k):
+        @pl.when(halos[k][1])
+        def _():
+            halos[k][0].start()
+
+    def halo_arrive(k):
+        @pl.when(halos[k][2])
+        def _():
+            halos[k][0].wait_recv()
+
+    halo_start(0)
+    halo_start(1)
     h_far = group(hg.at[pl.ds(0, 3)], *[(act, hg.at[f], at_z(d)) for d in (2, 4, 6)])
     h_near = group(hg.at[0], (act, hg.at[f], partner))
     h_pass = group(hg.at[pl.ds(0, 3)], *[(hg.at[(f + d) % 8], hg.at[(f + d) % 8], partner) for d in (2, 4, 6)])
@@ -214,7 +233,7 @@
         for copy in copies:
             copy.wait_send()
 
-    gather_slots = [slot() for _ in range(18)]
+    gather_slots = [slot() for _ in range(21)]
 
     class Gather:
         def __init__(self, buf):
@@ -225,7 +244,14 @@
                 return Group(gather_slots[count[0] - 1], like, *[(region, region, device) for region, device in moves])
 
             up, down, right, left = at_y(1), at_y(3), at_x(1), at_x(3)
-            self.zc = stage(rz, *[(buf.at[y, x, z, low_rows], at_z(d)) for d in range(1, 8)])
+            own = buf.at[y, x, z, low_rows]
+            flips = (1 - 2 * (z % 2), 2 - 4 * (z // 2 % 2), 4)
+
+            def across(k):
+                return at_z(8 + k % 2 * flips[0] + k // 2 % 2 * flips[1] + k // 4 * flips[2])
+
+            self.zc = stage(rz.at[pl.ds(0, 3)], *[(own, across(k)) for k in (2, 3, 1)])
+            self.zd = stage(rz.at[pl.ds(0, 4)], *[(own, across(k)) for k in (4, 5, 6, 7)])
             self.cx = stage(cxb, *[(buf.at[y, x, z, end], at_x(d)) for d in (1, 2, 3)])
             self.cy = stage(cyb, *[(buf.at[y, every, z, end], at_y(d)) for d in (1, 2, 3)])
             self.cz = []
@@ -239,14 +265,22 @@
                 self.cz.append(ring)
             two, four = buf.at[0, pl.ds(0, 2), every, lo], buf.at[0, every, every, lo]
             eight = buf.at[pl.ds(0, 2), every, every, lo]
-            a_own, b_own = buf.at[y, x, every, lo], buf.at[y, x, every, hi]
-            self.m1 = stage(four, (a_own, right), (a_own, left), (b_own, up), (b_own, down))
+            near, away = pl.ds(z // 4 * 4, 4), pl.ds(4 - z // 4 * 4, 4)
+
+            def sides(part, one, other):
+                return [(part, one), (part, other)]
+
+            a_near, b_near = buf.at[y, x, near, lo], buf.at[y, x, near, hi]
+            a_away, b_away = buf.at[y, x, away, lo], buf.at[y, x, away, hi]
+            self.m1 = stage(two, *(sides(a_near, right, left) + sides(b_near, up, down)))
+            self.n1 = stage(two, *(sides(a_away, right, left) + sides(b_away, up, down)))
             self.m2 = stage(
                 two,
                 (buf.at[y, xl, quad[0], lo], right), (buf.at[y, xr, quad[1], lo], left),
                 (buf.at[yl, x, quad[0], hi], up), (buf.at[yr, x, quad[1], hi], down),
             )
-            self.hp = stage(four, (a_own, up), (a_own, down), (b_own, right), (b_own, left))
+            self.hp = stage(two, *(sides(a_near, up, down) + sides(b_near, right, left)))
+            self.hq = stage(two, *(sides(a_away, up, down) + sides(b_away, right, left)))
 
             def bulk(xx, yy):
                 a_part, b_part = buf.at[y, xx, every, lo], buf.at[yy, x, every, hi]
@@ -261,18 +295,19 @@
                 (buf.at[yl, xl, every, hi], right), (buf.at[yr, xr, every, hi], left),
             )
             self.f3 = stage(two, (buf.at[yr, xo, every, lo], down), (buf.at[yo, xr, every, hi], left))
-            self.stages = [self.zc, self.cx, self.cy] + sum(self.cz, [])
+            self.stages = [self.zc, self.zd, self.n1, self.hq, self.cx, self.cy] + sum(self.cz, [])
             self.stages += [self.m1, self.m2, self.hp, self.hs, self.ho, self.f1, self.f2, self.f3]
 
         def event(self, k):
             after = {
-                1: (self.cx, self.cy), 2: (self.zc, self.m1, self.hp), 3: (self.cy, *self.cz[0]),
-                4: (self.m1, self.m2, self.hs), 5: (self.hp, self.f1), 7: (self.m2, self.ho),
-                9: (self.hs, self.f2), 11: (self.ho, self.f3),
+                1: ((self.cx,), (self.cy,)), 2: ((self.zc,), (self.m1, self.hp)), 3: ((self.cy,), self.cz[0]),
+                4: ((self.m1, self.n1), (self.m2, self.hs)), 5: ((self.hp, self.hq), (self.f1,)), 7: ((self.m2,), (self.ho,)),
+                9: ((self.hs,), (self.f2,)), 11: ((self.ho,), (self.f3,)), 14: ((self.zd,), (self.n1, self.hq)),
             }
             if k in after:
-                after[k][0].arrive()
-                for stage in after[k][1:]:
+                for stage in after[k][0]:
+                    stage.arrive()
+                for stage in after[k][1]:
                     stage.start()
             elif k in (6, 8, 10):
                 ring = k // 2 - 2
@@ -294,6 +329,7 @@
     w_gather = Gather(w)
     w_gather.cx.start()
     w_gather.zc.start()
+    w_gather.zd.start()
     s_slots = [slot() for _ in range(4)]
 
     def s_copy(group, index):
@@ -302,15 +338,21 @@
     def pair_step(group, p):
         n = group * 8 + 2 * p
         step = group * 4 + p
-        for when, event in ((3, 1), (5, 2), (6, 3), (8, 4), (10, 5), (11, 6), (12, 7), (14, 8)):
+        for when, event in ((2, 1), (3, 2), (5, 3), (6, 14), (8, 4), (9, 5), (10, 6), (11, 7), (13, 8)):
             @pl.when(step == when)
             def _(event=event):
                 w_gather.event(event)
 
-        @pl.when(step == 7)
+        @pl.when(step == 4)
         def _():
             h_far.arrive()
             h_pass.start()
+
+        for when, stage in ((2, 1), (4, 2), (6, 3), (8, 4)):
+            @pl.when(step == when)
+            def _(stage=stage):
+                halo_arrive(stage)
+                halo_start(stage + 1)
 
         win = window[...]
         h0, h1, h2 = sigv[n], sigv[n + 1], sigv[n + 2]
@@ -374,8 +416,19 @@
 
         @pl.when(group == 3)
         def _():
-            halo.wait_recv()
-            sigv[32] = sigv[32] * jnp.where(t * 8 + f == 255, 0.0, 1.0)
+            halo_arrive(0)
+            halo_arrive(5)
+            line = jnp.where(y < 3, 2, jnp.where(x < 3, 3, 4))
+            source = jnp.where(b == 0, 0, jnp.where(z_hi < 3, 1, line))
+            keep = jnp.where(t * 8 + f == 255, 0, 1)
+
+            @pl.when(keep == 1)
+            def _():
+                sigv[32] = hop[source]
+
+            @pl.when(keep == 0)
+            def _():
+                sigv[32] = jnp.zeros((256, 128), F32)
 
         def body(p, _):
             pair_step(group, p)
@@ -455,12 +508,14 @@
             return 0
 
         gather.event(12)
-        lax.fori_loop(0, 9, near_body, 0)
+        lax.fori_loop(0, 4, near_body, 0)
+        gather.event(11)
+        lax.fori_loop(4, 9, near_body, 0)
         gather.event(13)
         lax.fori_loop(0, 4, far_body, 0)
         lax.fori_loop(0, 3, side_body, 0)
 
-    for event in (9, 10, 11):
+    for event in (9, 10):
         w_gather.event(event)
     gain_all(w, lhs1, w_gather)
     gain1, mid_copy = gain((sx, rx), slot())
@@ -560,7 +615,6 @@
     w2.start(2, 3)
     chosen([(1, 1), (1, 0), (3, 3), (0, 1)])
     e1.start()
-    e2.start()
     chosen([(1, 3), (3, 1), (3, 0), (0, 3), (0, 0)])
 
     def zz(d):
@@ -592,6 +646,7 @@
     w1.arrive()
     pass_on((3, 1))
     l1.start()
+    e2.start()
     ring1.arrive()
     for side, place in ((0, zz(3)), (1, zz(-3))):
         target = num.at[half[side], every, place, end]
@@ -608,13 +663,13 @@
     ring_add(c2, 2)
     ring3 = ring_send(c3, 2)
     e1.arrive()
-    ring3.arrive()
-    ring_add(c3, 1)
-    ring4 = ring_send(c4, 1)
     l1.arrive()
     settle((3, 1))
     mf.start()
     me1.start()
+    ring3.arrive()
+    ring_add(c3, 1)
+    ring4 = ring_send(c4, 1)
     e2.arrive()
     l2.arrive()
     settle((2, 0))
@@ -660,10 +715,11 @@
         whole = whole + rz[d]
     wn[y, x, z, low_rows] = w[y, x, z, low_rows] * (whole / totals[:48])
     n_gather.zc.start()
+    n_gather.zd.start()
 
     out_templ[...] = moved(wn[y, x, z], perms[2 * flip + 1])
     acc[...] = jnp.zeros_like(acc)
-    for event in (1, 3, 2, 6, 4, 5, 7, 8, 9, 10, 11):
+    for event in (1, 2, 3, 14, 6, 4, 5, 7, 8, 9, 10):
         n_gather.event(event)
     gain_all(wn, mid_lhs, n_gather)
     gain2, last_copy = gain((sy, ry), slot())
@@ -678,7 +734,11 @@
     )
     f_copies.start()
     fo[pl.ds(z_hi, 1)] = fin[pl.ds(pl.multiple_of(8 * f, 8), 8), :][None]
-    halo.wait_send()
+    for copy, sends, _ in halos:
+        @pl.when(sends)
+        def _(copy=copy):
+            copy.wait_send()
+
     n_gather.all_sent()
     for g in range(4):
         s_copy(g, s_slots[g]).wait_send()
@@ -686,6 +746,7 @@
     for part in groups:
         part.sent()
     f_copies.arrive()
+    assert used[0] <= COPIES, used[0]
     out_act[...] = fo[...]
 
 
@@ -696,7 +757,7 @@
     out_templ[...] = templ[...]
 
 
-COPIES = 64
+COPIES = 57
 
 
 def on_device(signal, templates, activations):
@@ -735,6 +796,7 @@
             f32(3, 4, 16, 128),
             f32(3, 16, 128),
             f32(7, 48, 128),
+            f32(6, 256, 128),
             f32(144, 128),
             f32(72, 128), f32(72, 128), f32(72, 128), f32(72, 128),
             f32(8, 128),

time: 126 us -> 131 us (1.040)
  Pallas kernels: 125 us -> 130 us
    pallas_call x1, Pallas kernels: 124 us -> 129 us  [on_device(): pl.pallas_call(kernel, out_shape=(jax.ShapeDtypeStruct((4, 8, 128), F32),...]
where the time goes in v5:
time: 131 us
  Pallas kernels  130 us (99%)
    pallas_call x1, Pallas kernels, on_device(): pl.pallas_call(kernel, out_shape=(jax.ShapeDtypeStruct((4, 8, 128), F32),...  129 us

profile of v5, /device:TPU:1, one launch (start us, length us, event | category | flops | bytes accessed | tf_op | source)
XLA Modules:
  0.0 131.1 jit_solution(3396826644341500622)
XLA Ops:
  0.6 129.0 %shard_map.113 = (f32[4,8,128]{2,1,0:T(8,128)}, f32[64,128]{1,0:T(8,128)}) custom-call(f32[32,256,128]{2,1,0:T(8,128)} %bitcast.1, f32[64,128]{1,0:T(8,128)} %templ.1, f32[8,256]{1,0:T(8,128)} %act.1, f32[256,128]{1,0:T(8,128)} %constant.14.clone.window, f32[256,128]{1,0:T(8,128)} %constant.15.clone.tcos, f32[256,128]{1,0:T(8,128)} %constant.16.clone.tsin, ...), custom_call_target="tpu_custom_call" | custom-call | tf_op jit(solution)/shard_map/pallas_call | solution.py:767
  129.7 1.4 %shard_map.114 = (f32[8,256]{1,0:T(8,128)}, f32[64,128]{1,0:T(8,128)}) custom-call(f32[4,8,128]{2,1,0:T(8,128)} %get-tuple-element.4.parts, f32[64,128]{1,0:T(8,128)} %get-tuple-element.5.templ), custom_call_target="tpu_custom_call" | custom-call | tf_op jit(solution)/shard_map/pallas_call | solution.py:815

commit v6 on v5

--- a/solution.py
+++ b/solution.py
@@ -147,7 +147,6 @@
     w[y, x, z] = moved(templ[...], perms[2 * flip])
     hg[pl.ds(f, 1)] = act[...][None]
     zrow[...] = jnp.zeros_like(zrow)
-    pl.semaphore_wait(barrier, len(greet))
 
     used = [0]
 
@@ -205,13 +204,9 @@
         def _():
             halos[k][0].wait_recv()
 
-    halo_start(0)
-    halo_start(1)
     h_far = group(hg.at[pl.ds(0, 3)], *[(act, hg.at[f], at_z(d)) for d in (2, 4, 6)])
     h_near = group(hg.at[0], (act, hg.at[f], partner))
     h_pass = group(hg.at[pl.ds(0, 3)], *[(hg.at[(f + d) % 8], hg.at[(f + d) % 8], partner) for d in (2, 4, 6)])
-    h_far.start()
-    h_near.start()
 
     lo, hi, low_rows = pl.ds(0, 24), pl.ds(24, 24), pl.ds(0, 48)
     end = pl.ds(48, 16)
@@ -233,7 +228,7 @@
         for copy in copies:
             copy.wait_send()
 
-    gather_slots = [slot() for _ in range(21)]
+    gather_slots = [slot() for _ in range(18)]
 
     class Gather:
         def __init__(self, buf):
@@ -244,14 +239,7 @@
                 return Group(gather_slots[count[0] - 1], like, *[(region, region, device) for region, device in moves])
 
             up, down, right, left = at_y(1), at_y(3), at_x(1), at_x(3)
-            own = buf.at[y, x, z, low_rows]
-            flips = (1 - 2 * (z % 2), 2 - 4 * (z // 2 % 2), 4)
-
-            def across(k):
-                return at_z(8 + k % 2 * flips[0] + k // 2 % 2 * flips[1] + k // 4 * flips[2])
-
-            self.zc = stage(rz.at[pl.ds(0, 3)], *[(own, across(k)) for k in (2, 3, 1)])
-            self.zd = stage(rz.at[pl.ds(0, 4)], *[(own, across(k)) for k in (4, 5, 6, 7)])
+            self.zc = stage(rz, *[(buf.at[y, x, z, low_rows], at_z(d)) for d in range(1, 8)])
             self.cx = stage(cxb, *[(buf.at[y, x, z, end], at_x(d)) for d in (1, 2, 3)])
             self.cy = stage(cyb, *[(buf.at[y, every, z, end], at_y(d)) for d in (1, 2, 3)])
             self.cz = []
@@ -265,22 +253,14 @@
                 self.cz.append(ring)
             two, four = buf.at[0, pl.ds(0, 2), every, lo], buf.at[0, every, every, lo]
             eight = buf.at[pl.ds(0, 2), every, every, lo]
-            near, away = pl.ds(z // 4 * 4, 4), pl.ds(4 - z // 4 * 4, 4)
-
-            def sides(part, one, other):
-                return [(part, one), (part, other)]
-
-            a_near, b_near = buf.at[y, x, near, lo], buf.at[y, x, near, hi]
-            a_away, b_away = buf.at[y, x, away, lo], buf.at[y, x, away, hi]
-            self.m1 = stage(two, *(sides(a_near, right, left) + sides(b_near, up, down)))
-            self.n1 = stage(two, *(sides(a_away, right, left) + sides(b_away, up, down)))
+            a_own, b_own = buf.at[y, x, every, lo], buf.at[y, x, every, hi]
+            self.m1 = stage(four, (a_own, right), (a_own, left), (b_own, up), (b_own, down))
             self.m2 = stage(
                 two,
                 (buf.at[y, xl, quad[0], lo], right), (buf.at[y, xr, quad[1], lo], left),
                 (buf.at[yl, x, quad[0], hi], up), (buf.at[yr, x, quad[1], hi], down),
             )
-            self.hp = stage(two, *(sides(a_near, up, down) + sides(b_near, right, left)))
-            self.hq = stage(two, *(sides(a_away, up, down) + sides(b_away, right, left)))
+            self.hp = stage(four, (a_own, up), (a_own, down), (b_own, right), (b_own, left))
 
             def bulk(xx, yy):
                 a_part, b_part = buf.at[y, xx, every, lo], buf.at[yy, x, every, hi]
@@ -295,19 +275,18 @@
                 (buf.at[yl, xl, every, hi], right), (buf.at[yr, xr, every, hi], left),
             )
             self.f3 = stage(two, (buf.at[yr, xo, every, lo], down), (buf.at[yo, xr, every, hi], left))
-            self.stages = [self.zc, self.zd, self.n1, self.hq, self.cx, self.cy] + sum(self.cz, [])
+            self.stages = [self.zc, self.cx, self.cy] + sum(self.cz, [])
             self.stages += [self.m1, self.m2, self.hp, self.hs, self.ho, self.f1, self.f2, self.f3]
 
         def event(self, k):
             after = {
-                1: ((self.cx,), (self.cy,)), 2: ((self.zc,), (self.m1, self.hp)), 3: ((self.cy,), self.cz[0]),
-                4: ((self.m1, self.n1), (self.m2, self.hs)), 5: ((self.hp, self.hq), (self.f1,)), 7: ((self.m2,), (self.ho,)),
-                9: ((self.hs,), (self.f2,)), 11: ((self.ho,), (self.f3,)), 14: ((self.zd,), (self.n1, self.hq)),
+                1: (self.cx, self.cy), 2: (self.zc, self.m1, self.hp), 3: (self.cy, *self.cz[0]),
+                4: (self.m1, self.m2, self.hs), 5: (self.hp, self.f1), 7: (self.m2, self.ho),
+                9: (self.hs, self.f2), 11: (self.ho, self.f3),
             }
             if k in after:
-                for stage in after[k][0]:
-                    stage.arrive()
-                for stage in after[k][1]:
+                after[k][0].arrive()
+                for stage in after[k][1:]:
                     stage.start()
             elif k in (6, 8, 10):
                 ring = k // 2 - 2
@@ -327,33 +306,32 @@
                 stage.sent()
 
     w_gather = Gather(w)
-    w_gather.cx.start()
-    w_gather.zc.start()
-    w_gather.zd.start()
     s_slots = [slot() for _ in range(4)]
 
     def s_copy(group, index):
         return remote(tsend.at[group], sg.at[4 * b + group], index, partner)
 
-    def pair_step(group, p):
-        n = group * 8 + 2 * p
-        step = group * 4 + p
-        for when, event in ((2, 1), (3, 2), (5, 3), (6, 14), (8, 4), (9, 5), (10, 6), (11, 7), (13, 8)):
+    def exchange_step(step):
+        for when, event in ((7, 1), (9, 2), (10, 3), (12, 4), (14, 5), (15, 6)):
             @pl.when(step == when)
             def _(event=event):
                 w_gather.event(event)
 
-        @pl.when(step == 4)
+        @pl.when(step == 8)
         def _():
             h_far.arrive()
             h_pass.start()
 
-        for when, stage in ((2, 1), (4, 2), (6, 3), (8, 4)):
+        for when, stage in ((6, 1), (8, 2), (10, 3), (11, 4)):
             @pl.when(step == when)
             def _(stage=stage):
                 halo_arrive(stage)
                 halo_start(stage + 1)
 
+    def pair_step(group, p):
+        n = group * 8 + 2 * p
+        if not isinstance(group, int):
+            exchange_step(group * 4 + p)
         win = window[...]
         h0, h1, h2 = sigv[n], sigv[n + 1], sigv[n + 2]
         a0, a1 = h0 * win, h1 * win
@@ -401,11 +379,6 @@
                 ref[index, pl.ds(256 * place + j, 32, stride=8), :] = value[off + 32 * part:off + 32 * part + 32]
 
     def group_step(group, _):
-        @pl.when(group == 0)
-        def _():
-            loads[0].wait()
-            loads[1].wait()
-
         @pl.when(group == 1)
         def _():
             loads[2].wait()
@@ -430,6 +403,14 @@
             def _():
                 sigv[32] = jnp.zeros((256, 128), F32)
 
+        transform(group)
+        for g in range(1, 4):
+            @pl.when(group == g)
+            def _(g=g):
+                s_copy(g, s_slots[g]).start()
+        return 0
+
+    def transform(group):
         def body(p, _):
             pair_step(group, p)
             return 0
@@ -445,13 +426,19 @@
             return 0
 
         lax.fori_loop(0, 4, turn_body, 0)
-        for g in range(4):
-            @pl.when(group == g)
-            def _(g=g):
-                s_copy(g, s_slots[g]).start()
-        return 0
-
-    lax.fori_loop(0, 4, group_step, 0)
+
+    loads[0].wait()
+    loads[1].wait()
+    transform(0)
+    pl.semaphore_wait(barrier, len(greet))
+    w_gather.cx.start()
+    w_gather.zc.start()
+    h_far.start()
+    h_near.start()
+    halo_start(0)
+    halo_start(1)
+    s_copy(0, s_slots[0]).start()
+    lax.fori_loop(1, 4, group_step, 0)
 
     h_near.arrive()
     h_pass.arrive()
@@ -461,23 +448,23 @@
     for g in range(4):
         s_copy(g, s_slots[g]).wait_recv()
 
-    def frames_block(yy, xx):
+    def frames_block(places):
         cols = []
-        for k in range(8):
+        for yy, xx, k in places:
             place = pl.multiple_of(((yy * 4 + xx) * 8 + k) * 8, 8)
             cols.append(jnp.concatenate([sg[g, pl.ds(place, 8), :] for g in range(8)], 0))
         return jnp.concatenate(cols, 1)
 
-    def ratio_of(buf, lhs, yy, xx):
-        wide = jnp.concatenate([buf[yy, xx, k] for k in range(8)], 1)
+    def ratio_of(buf, lhs, places):
+        wide = jnp.concatenate([buf[place] for place in places], 1)
         high, low = split(wide)
         approx = dot(lhs, jnp.concatenate([high, high, low, low], 0))
-        return frames_block(yy, xx) / approx, high, low
-
-    def gain_block(buf, lhs, yy, xx):
-        ratio, high, low = ratio_of(buf, lhs, yy, xx)
+        return frames_block(places) / approx, high, low
+
+    def gain_block(buf, lhs, places):
+        ratio, high, low = ratio_of(buf, lhs, places)
         r_high, r_low = split(ratio)
-        left = jnp.concatenate([r_high, r_low, jnp.ones((16, 1024), BF16)], 0)
+        left = jnp.concatenate([r_high, r_low, jnp.ones((16, 128 * len(places)), BF16)], 0)
         acc[...] += dot_t(left, jnp.concatenate([high, low], 0))
 
     def gain(stage, index):
@@ -494,28 +481,26 @@
     lhs1 = doubled(h2)
     acc[...] = jnp.zeros_like(acc)
 
+    near = [(yy, xx) for yy in (yl, y, yr) for xx in (xl, x, xr)]
+    far = [(yo, xx) for xx in (xl, x, xr, xo)] + [(yy, xo) for yy in (yl, y, yr)]
+
     def gain_all(buf, lhs, gather):
-        def near_body(i, _):
-            gain_block(buf, lhs, (y + 3 + i // 3) % 4, (x + 3 + i % 3) % 4)
-            return 0
-
-        def far_body(i, _):
-            gain_block(buf, lhs, (y + 2) % 4, i)
-            return 0
-
-        def side_body(i, _):
-            gain_block(buf, lhs, (y + 3 + i) % 4, (x + 2) % 4)
-            return 0
-
+        def run_z(start, stop, which):
+            def body(i, _):
+                gain_block(buf, lhs, [(yy, xx, (z + i) % 8) for yy, xx in which])
+                return 0
+
+            lax.fori_loop(start, stop, body, 0)
+
+        run_z(5, 8, near)
+        gather.event(11)
+        run_z(8, 12, near)
         gather.event(12)
-        lax.fori_loop(0, 4, near_body, 0)
-        gather.event(11)
-        lax.fori_loop(4, 9, near_body, 0)
+        run_z(12, 13, near)
         gather.event(13)
-        lax.fori_loop(0, 4, far_body, 0)
-        lax.fori_loop(0, 3, side_body, 0)
-
-    for event in (9, 10):
+        run_z(0, 8, far)
+
+    for event in (7, 8, 9, 10):
         w_gather.event(event)
     gain_all(w, lhs1, w_gather)
     gain1, mid_copy = gain((sx, rx), slot())
@@ -529,7 +514,7 @@
     tx_copies.start()
 
     def num_block(yy, xx):
-        ratio, _, _ = ratio_of(w, mid_lhs, yy, xx)
+        ratio, _, _ = ratio_of(w, mid_lhs, [(yy, xx, k) for k in range(8)])
         high, low = split(ratio)
         out = dot(mid_left, jnp.concatenate([high, high, low, low], 0))
         for k in range(8):
@@ -715,11 +700,10 @@
         whole = whole + rz[d]
     wn[y, x, z, low_rows] = w[y, x, z, low_rows] * (whole / totals[:48])
     n_gather.zc.start()
-    n_gather.zd.start()
 
     out_templ[...] = moved(wn[y, x, z], perms[2 * flip + 1])
     acc[...] = jnp.zeros_like(acc)
-    for event in (1, 2, 3, 14, 6, 4, 5, 7, 8, 9, 10):
+    for event in (1, 3, 2, 6, 4, 5, 7, 8, 9, 10):
         n_gather.event(event)
     gain_all(wn, mid_lhs, n_gather)
     gain2, last_copy = gain((sy, ry), slot())
@@ -757,7 +741,7 @@
     out_templ[...] = templ[...]
 
 
-COPIES = 57
+COPIES = 54
 
 
 def on_device(signal, templates, activations):

time: 131 us -> 129 us (0.985)
    pallas_call x1, Pallas kernels: 129 us -> 127 us  [on_device(): pl.pallas_call(kernel, out_shape=(jax.ShapeDtypeStruct((4, 8, 128), F32),...]
where the time goes in v6:
time: 129 us
  Pallas kernels  129 us (100%)
    pallas_call x1, Pallas kernels, on_device(): pl.pallas_call(kernel, out_shape=(jax.ShapeDtypeStruct((4, 8, 128), F32),...  127 us

profile of v6, /device:TPU:1, one launch (start us, length us, event | category | flops | bytes accessed | tf_op | source)
XLA Modules:
  0.0 129.2 jit_solution(3073250215358457214)
XLA Ops:
  0.6 127.2 %shard_map.113 = (f32[4,8,128]{2,1,0:T(8,128)}, f32[64,128]{1,0:T(8,128)}) custom-call(f32[32,256,128]{2,1,0:T(8,128)} %bitcast.1, f32[64,128]{1,0:T(8,128)} %templ.1, f32[8,256]{1,0:T(8,128)} %act.1, f32[256,128]{1,0:T(8,128)} %constant.14.clone.window, f32[256,128]{1,0:T(8,128)} %constant.15.clone.tcos, f32[256,128]{1,0:T(8,128)} %constant.16.clone.tsin, ...), custom_call_target="tpu_custom_call" | custom-call | tf_op jit(solution)/shard_map/pallas_call | solution.py:751
  127.8 1.4 %shard_map.114 = (f32[8,256]{1,0:T(8,128)}, f32[64,128]{1,0:T(8,128)}) custom-call(f32[4,8,128]{2,1,0:T(8,128)} %get-tuple-element.4.parts, f32[64,128]{1,0:T(8,128)} %get-tuple-element.5.templ), custom_call_target="tpu_custom_call" | custom-call | tf_op jit(solution)/shard_map/pallas_call | solution.py:799

commit v7 on v3

--- a/solution.py
+++ b/solution.py
@@ -187,12 +187,9 @@
         return groups[-1]
 
     halo = remote(sig_hbm.at[0], sigv.at[32], slot(), at_line(-1))
-    halo.start()
     h_far = group(hg.at[pl.ds(0, 3)], *[(act, hg.at[f], at_z(d)) for d in (2, 4, 6)])
     h_near = group(hg.at[0], (act, hg.at[f], partner))
     h_pass = group(hg.at[pl.ds(0, 3)], *[(hg.at[(f + d) % 8], hg.at[(f + d) % 8], partner) for d in (2, 4, 6)])
-    h_far.start()
-    h_near.start()
 
     lo, hi, low_rows = pl.ds(0, 24), pl.ds(24, 24), pl.ds(0, 48)
     end = pl.ds(48, 16)
@@ -294,6 +291,9 @@
     w_gather = Gather(w)
     w_gather.cx.start()
     w_gather.zc.start()
+    h_far.start()
+    h_near.start()
+    halo.start()
     s_slots = [slot() for _ in range(4)]
 
     def s_copy(group, index):
@@ -408,23 +408,23 @@
     for g in range(4):
         s_copy(g, s_slots[g]).wait_recv()
 
-    def frames_block(yy, xx):
+    def frames_block(places):
         cols = []
-        for k in range(8):
+        for yy, xx, k in places:
             place = pl.multiple_of(((yy * 4 + xx) * 8 + k) * 8, 8)
             cols.append(jnp.concatenate([sg[g, pl.ds(place, 8), :] for g in range(8)], 0))
         return jnp.concatenate(cols, 1)
 
-    def ratio_of(buf, lhs, yy, xx):
-        wide = jnp.concatenate([buf[yy, xx, k] for k in range(8)], 1)
+    def ratio_of(buf, lhs, places):
+        wide = jnp.concatenate([buf[place] for place in places], 1)
         high, low = split(wide)
         approx = dot(lhs, jnp.concatenate([high, high, low, low], 0))
-        return frames_block(yy, xx) / approx, high, low
-
-    def gain_block(buf, lhs, yy, xx):
-        ratio, high, low = ratio_of(buf, lhs, yy, xx)
+        return frames_block(places) / approx, high, low
+
+    def gain_block(buf, lhs, places):
+        ratio, high, low = ratio_of(buf, lhs, places)
         r_high, r_low = split(ratio)
-        left = jnp.concatenate([r_high, r_low, jnp.ones((16, 1024), BF16)], 0)
+        left = jnp.concatenate([r_high, r_low, jnp.ones((16, 128 * len(places)), BF16)], 0)
         acc[...] += dot_t(left, jnp.concatenate([high, low], 0))
 
     def gain(stage, index):
@@ -441,26 +441,26 @@
     lhs1 = doubled(h2)
     acc[...] = jnp.zeros_like(acc)
 
+    near = [(yy, xx) for yy in (yl, y, yr) for xx in (xl, x, xr)]
+    far = [(yo, xx) for xx in (xl, x, xr, xo)] + [(yy, xo) for yy in (yl, y, yr)]
+
     def gain_all(buf, lhs, gather):
-        def near_body(i, _):
-            gain_block(buf, lhs, (y + 3 + i // 3) % 4, (x + 3 + i % 3) % 4)
-            return 0
-
-        def far_body(i, _):
-            gain_block(buf, lhs, (y + 2) % 4, i)
-            return 0
-
-        def side_body(i, _):
-            gain_block(buf, lhs, (y + 3 + i) % 4, (x + 2) % 4)
-            return 0
-
+        def run_z(start, stop, which):
+            def body(i, _):
+                gain_block(buf, lhs, [(yy, xx, (z + i) % 8) for yy, xx in which])
+                return 0
+
+            lax.fori_loop(start, stop, body, 0)
+
+        run_z(5, 8, near)
+        gather.event(11)
+        run_z(8, 12, near)
         gather.event(12)
-        lax.fori_loop(0, 9, near_body, 0)
+        run_z(12, 13, near)
         gather.event(13)
-        lax.fori_loop(0, 4, far_body, 0)
-        lax.fori_loop(0, 3, side_body, 0)
-
-    for event in (9, 10, 11):
+        run_z(0, 8, far)
+
+    for event in (9, 10):
         w_gather.event(event)
     gain_all(w, lhs1, w_gather)
     gain1, mid_copy = gain((sx, rx), slot())
@@ -474,7 +474,7 @@
     tx_copies.start()
 
     def num_block(yy, xx):
-        ratio, _, _ = ratio_of(w, mid_lhs, yy, xx)
+        ratio, _, _ = ratio_of(w, mid_lhs, [(yy, xx, k) for k in range(8)])
         high, low = split(ratio)
         out = dot(mid_left, jnp.concatenate([high, high, low, low], 0))
         for k in range(8):
@@ -560,7 +560,6 @@
     w2.start(2, 3)
     chosen([(1, 1), (1, 0), (3, 3), (0, 1)])
     e1.start()
-    e2.start()
     chosen([(1, 3), (3, 1), (3, 0), (0, 3), (0, 0)])
 
     def zz(d):
@@ -592,6 +591,7 @@
     w1.arrive()
     pass_on((3, 1))
     l1.start()
+    e2.start()
     ring1.arrive()
     for side, place in ((0, zz(3)), (1, zz(-3))):
         target = num.at[half[side], every, place, end]
@@ -608,13 +608,13 @@
     ring_add(c2, 2)
     ring3 = ring_send(c3, 2)
     e1.arrive()
-    ring3.arrive()
-    ring_add(c3, 1)
-    ring4 = ring_send(c4, 1)
     l1.arrive()
     settle((3, 1))
     mf.start()
     me1.start()
+    ring3.arrive()
+    ring_add(c3, 1)
+    ring4 = ring_send(c4, 1)
     e2.arrive()
     l2.arrive()
     settle((2, 0))
@@ -663,7 +663,7 @@
 
     out_templ[...] = moved(wn[y, x, z], perms[2 * flip + 1])
     acc[...] = jnp.zeros_like(acc)
-    for event in (1, 3, 2, 6, 4, 5, 7, 8, 9, 10, 11):
+    for event in (1, 3, 2, 6, 4, 5, 7, 8, 9, 10):
         n_gather.event(event)
     gain_all(wn, mid_lhs, n_gather)
     gain2, last_copy = gain((sy, ry), slot())

time: 126 us -> 122 us (0.968)
  Pallas kernels: 125 us -> 121 us
    pallas_call x1, Pallas kernels: 124 us -> 119 us  [on_device(): pl.pallas_call(kernel, out_shape=(jax.ShapeDtypeStruct((4, 8, 128), F32),...]
where the time goes in v7:
time: 122 us; the launch traced here: 121 us
  Pallas kernels  121 us (99%)
    pallas_call x1, Pallas kernels, on_device(): pl.pallas_call(kernel, out_shape=(jax.ShapeDtypeStruct((4, 8, 128), F32),...  119 us

profile of v7, /device:TPU:1, one launch (start us, length us, event | category | flops | bytes accessed | tf_op | source)
XLA Modules:
  0.0 121.4 jit_solution(3271422020471527235)
XLA Ops:
  0.6 119.4 %shard_map.113 = (f32[4,8,128]{2,1,0:T(8,128)}, f32[64,128]{1,0:T(8,128)}) custom-call(f32[32,256,128]{2,1,0:T(8,128)} %bitcast.1, f32[64,128]{1,0:T(8,128)} %templ.1, f32[8,256]{1,0:T(8,128)} %act.1, f32[256,128]{1,0:T(8,128)} %constant.14.clone.window, f32[256,128]{1,0:T(8,128)} %constant.15.clone.tcos, f32[256,128]{1,0:T(8,128)} %constant.16.clone.tsin, ...), custom_call_target="tpu_custom_call" | custom-call | tf_op jit(solution)/shard_map/pallas_call | solution.py:706
  120.0 1.4 %shard_map.114 = (f32[8,256]{1,0:T(8,128)}, f32[64,128]{1,0:T(8,128)}) custom-call(f32[4,8,128]{2,1,0:T(8,128)} %get-tuple-element.4.parts, f32[64,128]{1,0:T(8,128)} %get-tuple-element.5.templ), custom_call_target="tpu_custom_call" | custom-call | tf_op jit(solution)/shard_map/pallas_call | solution.py:753

commit v8 on v7

--- a/solution.py
+++ b/solution.py
@@ -302,7 +302,7 @@
     def pair_step(group, p):
         n = group * 8 + 2 * p
         step = group * 4 + p
-        for when, event in ((3, 1), (5, 2), (6, 3), (8, 4), (10, 5), (11, 6), (12, 7), (14, 8)):
+        for when, event in ((3, 1), (7, 3), (8, 2), (11, 6), (12, 4), (13, 5), (15, 7)):
             @pl.when(step == when)
             def _(event=event):
                 w_gather.event(event)
@@ -460,7 +460,7 @@
         gather.event(13)
         run_z(0, 8, far)
 
-    for event in (9, 10):
+    for event in (8, 9, 10):
         w_gather.event(event)
     gain_all(w, lhs1, w_gather)
     gain1, mid_copy = gain((sx, rx), slot())
@@ -686,6 +686,7 @@
     for part in groups:
         part.sent()
     f_copies.arrive()
+    assert used[0] <= COPIES, used[0]
     out_act[...] = fo[...]
 
 
@@ -696,7 +697,7 @@
     out_templ[...] = templ[...]
 
 
-COPIES = 64
+COPIES = 50
 
 
 def on_device(signal, templates, activations):

time: 122 us -> 121 us (level)
  no operation moved by 1% of the time
where the time goes in v8:
time: 121 us
  Pallas kernels  121 us (100%)
    pallas_call x1, Pallas kernels, on_device(): pl.pallas_call(kernel, out_shape=(jax.ShapeDtypeStruct((4, 8, 128), F32),...  119 us

profile of v8, /device:TPU:1, one launch (start us, length us, event | category | flops | bytes accessed | tf_op | source)
XLA Modules:
  0.0 121.2 jit_solution(3781711846857875162)
XLA Ops:
  0.6 119.2 %shard_map.113 = (f32[4,8,128]{2,1,0:T(8,128)}, f32[64,128]{1,0:T(8,128)}) custom-call(f32[32,256,128]{2,1,0:T(8,128)} %bitcast.1, f32[64,128]{1,0:T(8,128)} %templ.1, f32[8,256]{1,0:T(8,128)} %act.1, f32[256,128]{1,0:T(8,128)} %constant.14.clone.window, f32[256,128]{1,0:T(8,128)} %constant.15.clone.tcos, f32[256,128]{1,0:T(8,128)} %constant.16.clone.tsin, ...), custom_call_target="tpu_custom_call" | custom-call | tf_op jit(solution)/shard_map/pallas_call | solution.py:707
  119.8 1.4 %shard_map.114 = (f32[8,256]{1,0:T(8,128)}, f32[64,128]{1,0:T(8,128)}) custom-call(f32[4,8,128]{2,1,0:T(8,128)} %get-tuple-element.4.parts, f32[64,128]{1,0:T(8,128)} %get-tuple-element.5.templ), custom_call_target="tpu_custom_call" | custom-call | tf_op jit(solution)/shard_map/pallas_call | solution.py:754
